TPU v7x, 32 devices: a whole 2x2x4 slice. The times are simulated.
32 devices in a mesh: sub: 8 (over z, y), band: 4 (over x, core).
Axes of the slice: x: 2, y: 2, z: 4, core: 2. Of those that a mesh axis runs over, the one named last changes fastest.
Arguments:
- intensity: bfloat16 [4, 4096, 8192], P(None, ('band', 'sub')), may hold values from -6 to 6
- channel_spans: int32 [4096], replicated, may hold values from 1 to 8
Outputs:
- dedispersed: float32 [4, 512, 8192], P(None, ('band', 'sub'))
- peak_snr: float32 [4, 512, 8192], P(None, ('band', 'sub'))
All inputs are finite; a program needn't handle non-finite values.
Results may differ from a plain program's by a relative error of at most 0.0003.
Values sent between devices are 32-bit elements; how exact they have to be, the bound alone decides.
No kernel may reach another device: no remote copies, remote signals or barrier semaphores. Data moves between devices by JAX's collectives and lax.ppermute only.
A program may use at most 128 MiB of HBM per device.

v0:
```python
import functools
import math

import jax
import jax.numpy as jnp
from jax import lax
from jax.experimental import pallas as pl
from jax.experimental.pallas import tpu as pltpu
from jax.sharding import PartitionSpec as P

ROWS_DEV = 16
BOXES = 9
LANES = 128
HALF = ROWS_DEV // 2


def padding(longest_shift):
    return -(-(longest_shift // LANES + 1) // 8) * 8


def delayed(source, lead, row, shift, pad, tiles):
    coarse = shift // LANES
    fine = shift - coarse * LANES
    here = source[lead, row, pl.ds(pad - coarse, tiles), :]
    before = source[lead, row, pl.ds(pad - coarse - 1, tiles), :]
    lane = lax.broadcasted_iota(jnp.int32, (tiles, LANES), 1)
    mixed = jnp.where(lane < LANES - fine, here, before)
    return pltpu.roll(mixed, fine, 1)


def bit_of(number, position):
    return lax.shift_right_logical(number, jnp.int32(position)) & 1


def local_kernel(chan_dev, tiles, pad, info, spans, sums, power, keep, send, wide, level_a, level_b):
    device = info[0]
    groups = HALF
    span = chan_dev // groups
    zero = jnp.zeros((pad, LANES), jnp.float32)
    for m in range(1, groups, 2):
        for r in range(HALF):
            level_a[m, r, 0:pad, :] = zero
            level_b[m, r, 0:pad, :] = zero
    step = 1024 if (tiles * LANES) % 1024 == 0 else LANES
    for start in range(0, tiles * LANES, step):
        part = jnp.dot(
            sums[...], power[0, :, start : start + step], preferred_element_type=jnp.float32
        )
        for piece in range(step // LANES):
            wide[start // LANES + piece] = part[:, piece * LANES : (piece + 1) * LANES]
    for m in range(groups):
        level_a[m, 0, pad : pad + tiles, :] = wide[:, m, :]
    widths = []
    for m in range(groups):
        total = spans[device * chan_dev + m * span]
        for c in range(1, span):
            total = total + spans[device * chan_dev + m * span + c]
        widths.append(total)
    source, target = level_a, level_b
    rows = 4
    bands = groups // 2
    old_rows = 1
    while True:
        last = rows == ROWS_DEV
        merged = []
        for m in range(bands):
            low, both = widths[2 * m], widths[2 * m] + widths[2 * m + 1]
            merged.append(both)
            if last:
                mine = bit_of(device, 0)
                for half, ref in ((mine, keep), (1 - mine, send)):

                    def body(i, carry, half=half, ref=ref, low=low, both=both, source=source):
                        r = half * HALF + i
                        shift = (r * low) // both
                        q = r // 2
                        ref[0, i] = source[0, q, pad : pad + tiles, :] + delayed(
                            source, 1, q, shift, pad, tiles
                        )
                        return carry

                    lax.fori_loop(0, HALF, body, 0)
            else:
                for r in range(rows):
                    q = r * old_rows // rows
                    shift = (r * low) // both
                    result = source[2 * m, q, pad : pad + tiles, :]
                    if r < 2:
                        result = result + source[2 * m + 1, q, pad : pad + tiles, :]
                    else:
                        result = result + delayed(source, 2 * m + 1, q, shift, pad, tiles)
                    target[m, r, pad : pad + tiles, :] = result
        if last:
            break
        widths = merged
        source, target = target, source
        old_rows, rows, bands = rows, rows * 2, bands // 2


def merge_rows(step, tiles, pad, info, kept, came, held, sems):
    device = info[0]
    mine = bit_of(device, step)
    copies = [
        pltpu.make_async_copy(kept.at[0], held.at[mine, :, pl.ds(pad, tiles), :], sems.at[0]),
        pltpu.make_async_copy(came.at[0], held.at[1 - mine, :, pl.ds(pad, tiles), :], sems.at[1]),
    ]
    for copy in copies:
        copy.start()
    zero = jnp.zeros((pad, LANES), jnp.float32)
    for q in range(HALF):
        held[1, q, 0:pad, :] = zero
    block = jnp.int32(0)
    for position in range(step + 1):
        block = 2 * block + bit_of(device, position)
    size = 2**step
    first = (device // (2 * size)) * (2 * size)
    low = info[1 + first + size] - info[1 + first]
    both = info[1 + first + 2 * size] - info[1 + first]
    for copy in copies:
        copy.wait()

    def row(i):
        shift = ((block * ROWS_DEV + i) * low) // both
        q = i // 2
        return held[0, q, pl.ds(pad, tiles), :] + delayed(held, 1, q, shift, pad, tiles)

    return row


def merge_kernel(step, tiles, pad, info, kept, came, keep, send, held, sems):
    row = merge_rows(step, tiles, pad, info, kept, came, held, sems)
    following = bit_of(info[0], step + 1)
    for half, ref in ((1 - following, send), (following, keep)):

        def body(i, carry, half=half, ref=ref):
            ref[0, i] = row(half * HALF + i)
            return carry

        lax.fori_loop(0, HALF, body, 0)


def final_kernel(step, tiles, pad, scale, *refs):
    info, kept, came = refs[:3]
    plane, peak, held, flat, tops, sems = refs[-6:]
    row = merge_rows(step, tiles, pad, info, kept, came, held, sems)
    lane = lax.broadcasted_iota(jnp.int32, (tiles, LANES), 1)
    first = lax.broadcasted_iota(jnp.int32, (tiles, LANES), 0) == 0

    def body(i, carry):
        running = row(i) * scale
        flat[i] = running
        best = running
        width = 1
        for _ in range(BOXES - 1):
            before = jnp.where(first, 0.0, pltpu.roll(running, 1, 0))
            if width < LANES:
                mixed = jnp.where(lane < LANES - width, running, before)
                running = running + pltpu.roll(mixed, width, 1)
            else:
                running = running + before
            width = width * 2
            best = jnp.maximum(best, running * (1.0 / math.sqrt(width)))
        tops[i] = best
        return carry

    lax.fori_loop(0, ROWS_DEV, body, 0)
    for h in range(0, ROWS_DEV, 8):

        def out(j, carry, h=h):
            columns = pl.ds(pl.multiple_of(j * LANES, LANES), LANES)
            plane[0, h : h + 8, columns] = flat[h : h + 8, j, :]
            peak[0, h : h + 8, columns] = tops[h : h + 8, j, :]
            return carry

        lax.fori_loop(0, tiles, out, 0)


SMEM = pl.BlockSpec(memory_space=pltpu.SMEM)
HBM = pl.BlockSpec(memory_space=pltpu.HBM)


def swapped(value, axis, distance):
    mask = 2**distance
    return lax.ppermute(value, axis, [(s, s ^ mask) for s in range(lax.axis_size(axis))])


def on_device(intensity, channel_spans):
    beams, chan_dev, samples = intensity.shape
    sub_count = lax.axis_size("sub")
    band_size = lax.axis_size("band")
    devices = sub_count * band_size
    tiles = samples // LANES
    sub_bits = sub_count.bit_length() - 1
    bits = devices.bit_length() - 1
    device = lax.axis_index("band") * sub_count + lax.axis_index("sub")
    totals = channel_spans.reshape(devices, chan_dev).sum(axis=1)
    edge = jnp.arange(devices + 1)[:, None] > jnp.arange(devices)[None, :]
    edges = jnp.where(edge, totals[None, :], 0).sum(axis=1)
    info = jnp.concatenate([device.reshape(1), edges]).astype(jnp.int32)
    place = device.reshape(1).astype(jnp.int32)
    group = jnp.arange(chan_dev) // (chan_dev // HALF)
    sums = (jnp.arange(HALF)[:, None] == group[None, :]).astype(jnp.bfloat16)
    halves = jax.ShapeDtypeStruct((1, HALF, tiles, LANES), jnp.float32)
    whole = jax.ShapeDtypeStruct((beams, ROWS_DEV, samples), jnp.float32)
    block = pl.BlockSpec((1, HALF, tiles, LANES), lambda i: (0, 0, 0, 0))
    size = HALF * tiles * LANES

    def local(beam):
        pad = padding(ROWS_DEV)
        return pl.pallas_call(
            functools.partial(local_kernel, chan_dev, tiles, pad),
            grid=(1,),
            in_specs=[
                SMEM,
                SMEM,
                pl.BlockSpec((HALF, chan_dev), lambda i: (0, 0)),
                pl.BlockSpec((1, chan_dev, samples), lambda i: (beam, 0, 0)),
            ],
            out_specs=[block, block],
            out_shape=[halves, halves],
            scratch_shapes=[
                pltpu.VMEM((tiles, HALF, LANES), jnp.float32),
                pltpu.VMEM((HALF, HALF, pad + tiles, LANES), jnp.float32),
                pltpu.VMEM((HALF, HALF, pad + tiles, LANES), jnp.float32),
            ],
            cost_estimate=pl.CostEstimate(
                flops=size * 40, bytes_accessed=chan_dev * samples * 2 + size * 8, transcendentals=0
            ),
            name="local",
        )(place, channel_spans, sums, intensity)

    def merge(step, kept, came):
        pad = padding(ROWS_DEV * 2 ** (step + 1))
        return pl.pallas_call(
            functools.partial(merge_kernel, step, tiles, pad),
            grid=(1,),
            in_specs=[SMEM, HBM, HBM],
            out_specs=[block, block],
            out_shape=[halves, halves],
            scratch_shapes=[
                pltpu.VMEM((2, HALF, pad + tiles, LANES), jnp.float32),
                pltpu.SemaphoreType.DMA((2,)),
            ],
            cost_estimate=pl.CostEstimate(
                flops=size * 8, bytes_accessed=size * 16, transcendentals=0
            ),
            name=f"merge{step}",
        )(info, kept, came)

    def final(beam, kept, came, done):
        step = bits - 1
        pad = padding(ROWS_DEV * 2**bits)
        rows = pl.BlockSpec((1, ROWS_DEV, samples), lambda i: (beam, 0, 0))
        return pl.pallas_call(
            functools.partial(
                final_kernel, step, tiles, pad, 1.0 / math.sqrt(chan_dev * devices)
            ),
            grid=(1,),
            in_specs=[SMEM, HBM, HBM] + [HBM] * len(done),
            out_specs=[rows, rows],
            out_shape=[whole, whole],
            scratch_shapes=[
                pltpu.VMEM((2, HALF, pad + tiles, LANES), jnp.float32),
                pltpu.VMEM((ROWS_DEV, tiles, LANES), jnp.float32),
                pltpu.VMEM((ROWS_DEV, tiles, LANES), jnp.float32),
                pltpu.SemaphoreType.DMA((2,)),
            ],
            input_output_aliases={3 + i: i for i in range(len(done))},
            cost_estimate=pl.CostEstimate(
                flops=size * 80, bytes_accessed=size * 24, transcendentals=0
            ),
            name="final",
        )(info, kept, came, *done)

    state = [local(beam) for beam in range(beams)]
    for step in range(bits):
        axis, distance = ("sub", step) if step < sub_bits else ("band", step - sub_bits)
        came = [swapped(send, axis, distance) for _, send in state]
        if step < bits - 1:
            state = [merge(step, state[b][0], came[b]) for b in range(beams)]
    done = ()
    for beam in range(beams):
        done = final(beam, state[beam][0], came[beam], done)
    return tuple(done)


def solution(mesh):
    spec = P(None, ("band", "sub"), None)
    return jax.shard_map(
        on_device, mesh=mesh, in_specs=(spec, P()), out_specs=(spec, spec), check_vma=False
    )
```

profile of v0, /device:TPU:0, one launch (start us, length us, event | category | flops | bytes accessed | tf_op | source)
XLA Modules:
  0.0 184.9 jit_solution(11000305954300731955)
XLA Ops:
  1.2 4.5 %local.7 = (f32[1,8,64,128]{3,2,1,0:T(8,128)}, f32[1,8,64,128]{3,2,1,0:T(8,128)}) custom-call(s32[1]{0:T(128)} %bitcast.info, s32[4096]{0:T(1024)} %spans.7, bf16[8,128]{1,0:T(8,128)(2,1)} %fusion.sums, bf16[4,128,8192]{2,1,0:T(8,128)(2,1)} %power.7), custom_call_target="tpu_custom_call" | custom-call | flops 2621440 | bytes 2621440 | tf_op jit(solution)/shard_map/local/pallas_call | solution.py:210
  5.7 3.0 %collective-permute-start.15 = (f32[1,8,64,128]{3,2,1,0:T(8,128)}, f32[1,8,64,128]{3,2,1,0:T(8,128)S(1)}, u32[]{:S(2)}, u32[]{:S(2)}) collective-permute-start(f32[1,8,64,128]{3,2,1,0:T(8,128)} %get-tuple-element.79), channel_id=1, source_target_pairs={{0,4},{4,0},{8,12},{12,8},{16,20},{20,16},{24,28},{28,24},{1,5},{5... | collective-permute-start | bytes 786440 | tf_op jit(solution)/shard_map/ppermute | solution.py:184
  8.7 4.5 %local.6 = (f32[1,8,64,128]{3,2,1,0:T(8,128)}, f32[1,8,64,128]{3,2,1,0:T(8,128)}) custom-call(s32[1]{0:T(128)} %bitcast.info, s32[4096]{0:T(1024)} %spans.7, bf16[8,128]{1,0:T(8,128)(2,1)} %fusion.sums, bf16[4,128,8192]{2,1,0:T(8,128)(2,1)} %power.7), custom_call_target="tpu_custom_call" | custom-call | flops 2621440 | bytes 2621440 | tf_op jit(solution)/shard_map/local/pallas_call | solution.py:210
  13.2 4.5 %local.5 = (f32[1,8,64,128]{3,2,1,0:T(8,128)}, f32[1,8,64,128]{3,2,1,0:T(8,128)}) custom-call(s32[1]{0:T(128)} %bitcast.info, s32[4096]{0:T(1024)} %spans.7, bf16[8,128]{1,0:T(8,128)(2,1)} %fusion.sums, bf16[4,128,8192]{2,1,0:T(8,128)(2,1)} %power.7), custom_call_target="tpu_custom_call" | custom-call | flops 2621440 | bytes 2621440 | tf_op jit(solution)/shard_map/local/pallas_call | solution.py:210
  17.7 2.0 %collective-permute-start.5 = (f32[1,8,64,128]{3,2,1,0:T(8,128)}, f32[1,8,64,128]{3,2,1,0:T(8,128)S(1)}, u32[]{:S(2)}, u32[]{:S(2)}) collective-permute-start(f32[1,8,64,128]{3,2,1,0:T(8,128)} %get-tuple-element.59), channel_id=1, source_target_pairs={{0,4},{4,0},{8,12},{12,8},{16,20},{20,16},{24,28},{28,24},{1,5},{5... | collective-permute-start | bytes 786440 | tf_op jit(solution)/shard_map/ppermute | solution.py:184
  19.7 4.4 %local.4 = (f32[1,8,64,128]{3,2,1,0:T(8,128)}, f32[1,8,64,128]{3,2,1,0:T(8,128)}) custom-call(s32[1]{0:T(128)} %bitcast.info, s32[4096]{0:T(1024)} %spans.7, bf16[8,128]{1,0:T(8,128)(2,1)} %fusion.sums, bf16[4,128,8192]{2,1,0:T(8,128)(2,1)} %power.7), custom_call_target="tpu_custom_call" | custom-call | flops 2621440 | bytes 2621440 | tf_op jit(solution)/shard_map/local/pallas_call | solution.py:210
  25.6 3.7 %merge0.7 = (f32[1,8,64,128]{3,2,1,0:T(8,128)}, f32[1,8,64,128]{3,2,1,0:T(8,128)}) custom-call(s32[34]{0:T(128)} %pad_add_fusion.info.refs_0_, f32[1,8,64,128]{3,2,1,0:T(8,128)} %get-tuple-element.78.kept, f32[1,8,64,128]{3,2,1,0:T(8,128)} %copy-done.20), custom_call_target="tpu_custom_call" | custom-call | flops 524288 | bytes 1048576 | tf_op jit(solution)/shard_map/merge0/pallas_call | solution.py:234
  29.4 2.1 %collective-permute-start.16 = (f32[1,8,64,128]{3,2,1,0:T(8,128)}, f32[1,8,64,128]{3,2,1,0:T(8,128)S(1)}, u32[]{:S(2)}, u32[]{:S(2)}) collective-permute-start(f32[1,8,64,128]{3,2,1,0:T(8,128)} %get-tuple-element.81), channel_id=1, source_target_pairs={{0,8},{4,12},{8,0},{12,4},{16,24},{20,28},{24,16},{28,20},{1,9},{5... | collective-permute-start | bytes 786440 | tf_op jit(solution)/shard_map/ppermute | solution.py:184
  32.2 3.7 %merge0.6 = (f32[1,8,64,128]{3,2,1,0:T(8,128)}, f32[1,8,64,128]{3,2,1,0:T(8,128)}) custom-call(s32[34]{0:T(128)} %pad_add_fusion.info.refs_0_, f32[1,8,64,128]{3,2,1,0:T(8,128)} %get-tuple-element.68.kept, f32[1,8,64,128]{3,2,1,0:T(8,128)} %copy-done.19), custom_call_target="tpu_custom_call" | custom-call | flops 524288 | bytes 1048576 | tf_op jit(solution)/shard_map/merge0/pallas_call | solution.py:234
  36.8 3.7 %merge0.5 = (f32[1,8,64,128]{3,2,1,0:T(8,128)}, f32[1,8,64,128]{3,2,1,0:T(8,128)}) custom-call(s32[34]{0:T(128)} %pad_add_fusion.info.refs_0_, f32[1,8,64,128]{3,2,1,0:T(8,128)} %get-tuple-element.58.kept, f32[1,8,64,128]{3,2,1,0:T(8,128)} %copy-done.5), custom_call_target="tpu_custom_call" | custom-call | flops 524288 | bytes 1048576 | tf_op jit(solution)/shard_map/merge0/pallas_call | solution.py:234
  40.5 2.1 %collective-permute-start.6 = (f32[1,8,64,128]{3,2,1,0:T(8,128)}, f32[1,8,64,128]{3,2,1,0:T(8,128)S(1)}, u32[]{:S(2)}, u32[]{:S(2)}) collective-permute-start(f32[1,8,64,128]{3,2,1,0:T(8,128)} %get-tuple-element.61), channel_id=1, source_target_pairs={{0,8},{4,12},{8,0},{12,4},{16,24},{20,28},{24,16},{28,20},{1,9},{5... | collective-permute-start | bytes 786440 | tf_op jit(solution)/shard_map/ppermute | solution.py:184
  42.6 0.7 copy-done.4
  43.3 3.7 %merge0.4 = (f32[1,8,64,128]{3,2,1,0:T(8,128)}, f32[1,8,64,128]{3,2,1,0:T(8,128)}) custom-call(s32[34]{0:T(128)} %pad_add_fusion.info.refs_0_, f32[1,8,64,128]{3,2,1,0:T(8,128)} %get-tuple-element.48.kept, f32[1,8,64,128]{3,2,1,0:T(8,128)} %copy-done.4), custom_call_target="tpu_custom_call" | custom-call | flops 524288 | bytes 1048576 | tf_op jit(solution)/shard_map/merge0/pallas_call | solution.py:234
  47.8 3.7 %merge1.7 = (f32[1,8,64,128]{3,2,1,0:T(8,128)}, f32[1,8,64,128]{3,2,1,0:T(8,128)}) custom-call(s32[34]{0:T(128)} %pad_add_fusion.info.refs_0_, f32[1,8,64,128]{3,2,1,0:T(8,128)} %get-tuple-element.80.kept, f32[1,8,64,128]{3,2,1,0:T(8,128)} %copy-done.6), custom_call_target="tpu_custom_call" | custom-call | flops 524288 | bytes 1048576 | tf_op jit(solution)/shard_map/merge1/pallas_call | solution.py:234
  51.5 3.1 %collective-permute-start.17 = (f32[1,8,64,128]{3,2,1,0:T(8,128)}, f32[1,8,64,128]{3,2,1,0:T(8,128)S(1)}, u32[]{:S(2)}, u32[]{:S(2)}) collective-permute-start(f32[1,8,64,128]{3,2,1,0:T(8,128)} %get-tuple-element.83), channel_id=1, source_target_pairs={{0,16},{4,20},{8,24},{12,28},{16,0},{20,4},{24,8},{28,12},{1,17},{... | collective-permute-start | bytes 786440 | tf_op jit(solution)/shard_map/ppermute | solution.py:184
  54.6 0.7 copy-done.7
  55.3 3.7 %merge1.6 = (f32[1,8,64,128]{3,2,1,0:T(8,128)}, f32[1,8,64,128]{3,2,1,0:T(8,128)}) custom-call(s32[34]{0:T(128)} %pad_add_fusion.info.refs_0_, f32[1,8,64,128]{3,2,1,0:T(8,128)} %get-tuple-element.70.kept, f32[1,8,64,128]{3,2,1,0:T(8,128)} %copy-done.7), custom_call_target="tpu_custom_call" | custom-call | flops 524288 | bytes 1048576 | tf_op jit(solution)/shard_map/merge1/pallas_call | solution.py:234
  59.8 3.7 %merge1.5 = (f32[1,8,64,128]{3,2,1,0:T(8,128)}, f32[1,8,64,128]{3,2,1,0:T(8,128)}) custom-call(s32[34]{0:T(128)} %pad_add_fusion.info.refs_0_, f32[1,8,64,128]{3,2,1,0:T(8,128)} %get-tuple-element.60.kept, f32[1,8,64,128]{3,2,1,0:T(8,128)} %copy-done.8), custom_call_target="tpu_custom_call" | custom-call | flops 524288 | bytes 1048576 | tf_op jit(solution)/shard_map/merge1/pallas_call | solution.py:234
  63.5 3.0 %collective-permute-start.7 = (f32[1,8,64,128]{3,2,1,0:T(8,128)}, f32[1,8,64,128]{3,2,1,0:T(8,128)S(1)}, u32[]{:S(2)}, u32[]{:S(2)}) collective-permute-start(f32[1,8,64,128]{3,2,1,0:T(8,128)} %get-tuple-element.63), channel_id=1, source_target_pairs={{0,16},{4,20},{8,24},{12,28},{16,0},{20,4},{24,8},{28,12},{1,17},{... | collective-permute-start | bytes 786440 | tf_op jit(solution)/shard_map/ppermute | solution.py:184
  66.5 0.7 copy-done.9
  67.2 3.7 %merge1.4 = (f32[1,8,64,128]{3,2,1,0:T(8,128)}, f32[1,8,64,128]{3,2,1,0:T(8,128)}) custom-call(s32[34]{0:T(128)} %pad_add_fusion.info.refs_0_, f32[1,8,64,128]{3,2,1,0:T(8,128)} %get-tuple-element.50.kept, f32[1,8,64,128]{3,2,1,0:T(8,128)} %copy-done.9), custom_call_target="tpu_custom_call" | custom-call | flops 524288 | bytes 1048576 | tf_op jit(solution)/shard_map/merge1/pallas_call | solution.py:234
  71.0 12.4 %collective-permute-done.17.came = f32[1,8,64,128]{3,2,1,0:T(8,128)S(1)} collective-permute-done((f32[1,8,64,128]{3,2,1,0:T(8,128)}, f32[1,8,64,128]{3,2,1,0:T(8,128)S(1)}, u32[]{:S(2)}, u32[]{:S(2)}) %collective-permute-start.17) | collective-permute-done | bytes 262176 | tf_op jit(solution)/shard_map/ppermute | solution.py:184
  83.4 0.7 copy-done.10
  84.1 3.7 %merge2.7 = (f32[1,8,64,128]{3,2,1,0:T(8,128)}, f32[1,8,64,128]{3,2,1,0:T(8,128)}) custom-call(s32[34]{0:T(128)} %pad_add_fusion.info.refs_0_, f32[1,8,64,128]{3,2,1,0:T(8,128)} %get-tuple-element.82.kept, f32[1,8,64,128]{3,2,1,0:T(8,128)} %copy-done.10), custom_call_target="tpu_custom_call" | custom-call | flops 524288 | bytes 1048576 | tf_op jit(solution)/shard_map/merge2/pallas_call | solution.py:234
  87.9 1.1 collective-permute-done.12.came
  89.0 0.7 copy-done.11
  89.7 3.7 %merge2.6 = (f32[1,8,64,128]{3,2,1,0:T(8,128)}, f32[1,8,64,128]{3,2,1,0:T(8,128)}) custom-call(s32[34]{0:T(128)} %pad_add_fusion.info.refs_0_, f32[1,8,64,128]{3,2,1,0:T(8,128)} %get-tuple-element.72.kept, f32[1,8,64,128]{3,2,1,0:T(8,128)} %copy-done.11), custom_call_target="tpu_custom_call" | custom-call | flops 524288 | bytes 1048576 | tf_op jit(solution)/shard_map/merge2/pallas_call | solution.py:234
  93.5 1.1 collective-permute-done.7.came
  94.6 0.7 copy-done.12
  95.4 3.7 %merge2.5 = (f32[1,8,64,128]{3,2,1,0:T(8,128)}, f32[1,8,64,128]{3,2,1,0:T(8,128)}) custom-call(s32[34]{0:T(128)} %pad_add_fusion.info.refs_0_, f32[1,8,64,128]{3,2,1,0:T(8,128)} %get-tuple-element.62.kept, f32[1,8,64,128]{3,2,1,0:T(8,128)} %copy-done.12), custom_call_target="tpu_custom_call" | custom-call | flops 524288 | bytes 1048576 | tf_op jit(solution)/shard_map/merge2/pallas_call | solution.py:234
  99.9 3.7 %merge2.4 = (f32[1,8,64,128]{3,2,1,0:T(8,128)}, f32[1,8,64,128]{3,2,1,0:T(8,128)}) custom-call(s32[34]{0:T(128)} %pad_add_fusion.info.refs_0_, f32[1,8,64,128]{3,2,1,0:T(8,128)} %get-tuple-element.52.kept, f32[1,8,64,128]{3,2,1,0:T(8,128)} %copy-done.13), custom_call_target="tpu_custom_call" | custom-call | flops 524288 | bytes 1048576 | tf_op jit(solution)/shard_map/merge2/pallas_call | solution.py:234
  104.2 0.7 copy-done.14
  104.9 3.7 %merge3.7 = (f32[1,8,64,128]{3,2,1,0:T(8,128)}, f32[1,8,64,128]{3,2,1,0:T(8,128)}) custom-call(s32[34]{0:T(128)} %pad_add_fusion.info.refs_0_, f32[1,8,64,128]{3,2,1,0:T(8,128)} %get-tuple-element.84.kept, f32[1,8,64,128]{3,2,1,0:T(8,128)} %copy-done.14), custom_call_target="tpu_custom_call" | custom-call | flops 524288 | bytes 1048576 | tf_op jit(solution)/shard_map/merge3/pallas_call | solution.py:234
  108.6 1.7 collective-permute-start.19
  110.3 0.7 copy-done.15
  111.0 3.7 %merge3.6 = (f32[1,8,64,128]{3,2,1,0:T(8,128)}, f32[1,8,64,128]{3,2,1,0:T(8,128)}) custom-call(s32[34]{0:T(128)} %pad_add_fusion.info.refs_0_, f32[1,8,64,128]{3,2,1,0:T(8,128)} %get-tuple-element.74.kept, f32[1,8,64,128]{3,2,1,0:T(8,128)} %copy-done.15), custom_call_target="tpu_custom_call" | custom-call | flops 524288 | bytes 1048576 | tf_op jit(solution)/shard_map/merge3/pallas_call | solution.py:234
  115.2 0.7 copy-done.16
  115.9 3.7 %merge3.5 = (f32[1,8,64,128]{3,2,1,0:T(8,128)}, f32[1,8,64,128]{3,2,1,0:T(8,128)}) custom-call(s32[34]{0:T(128)} %pad_add_fusion.info.refs_0_, f32[1,8,64,128]{3,2,1,0:T(8,128)} %get-tuple-element.64.kept, f32[1,8,64,128]{3,2,1,0:T(8,128)} %copy-done.16), custom_call_target="tpu_custom_call" | custom-call | flops 524288 | bytes 1048576 | tf_op jit(solution)/shard_map/merge3/pallas_call | solution.py:234
  119.6 1.7 collective-permute-start.9
  121.4 0.7 copy-done.17
  122.1 3.7 %merge3.4 = (f32[1,8,64,128]{3,2,1,0:T(8,128)}, f32[1,8,64,128]{3,2,1,0:T(8,128)}) custom-call(s32[34]{0:T(128)} %pad_add_fusion.info.refs_0_, f32[1,8,64,128]{3,2,1,0:T(8,128)} %get-tuple-element.54.kept, f32[1,8,64,128]{3,2,1,0:T(8,128)} %copy-done.17), custom_call_target="tpu_custom_call" | custom-call | flops 524288 | bytes 1048576 | tf_op jit(solution)/shard_map/merge3/pallas_call | solution.py:234
  126.2 0.7 copy-done.18
  126.9 14.0 %final.4 = (f32[4,16,8192]{2,1,0:T(8,128)}, f32[4,16,8192]{2,1,0:T(8,128)}) custom-call(s32[34]{0:T(128)} %pad_add_fusion.info.refs_0_, f32[1,8,64,128]{3,2,1,0:T(8,128)} %get-tuple-element.86.refs_1_, f32[1,8,64,128]{3,2,1,0:T(8,128)} %copy-done.18), custom_call_target="tpu_custom_call" | custom-call | flops 5242880 | bytes 1572864 | tf_op jit(solution)/shard_map/final/pallas_call | solution.py:254
  140.9 0.7 copy-done.1
  141.6 14.0 %final.5 = (f32[4,16,8192]{2,1,0:T(8,128)}, f32[4,16,8192]{2,1,0:T(8,128)}) custom-call(s32[34]{0:T(128)} %pad_add_fusion.info.refs_0_, f32[1,8,64,128]{3,2,1,0:T(8,128)} %get-tuple-element.76.refs_1_, f32[1,8,64,128]{3,2,1,0:T(8,128)} %copy-done.1, f32[4,16,8192]{2,1,0:T(8,128)} %get-tuple-element.88.refs_3_, ...), custom_call_target="tpu_custom_call", output_to_operand_aliasing={{0}: (3, {}), {1}: (4, {})} | custom-call | flops 5242880 | bytes 1572864 | tf_op jit(solution)/shard_map/final/pallas_call | solution.py:254
  155.6 0.7 copy-done.2
  156.3 14.0 %final.6 = (f32[4,16,8192]{2,1,0:T(8,128)}, f32[4,16,8192]{2,1,0:T(8,128)}) custom-call(s32[34]{0:T(128)} %pad_add_fusion.info.refs_0_, f32[1,8,64,128]{3,2,1,0:T(8,128)} %get-tuple-element.66.refs_1_, f32[1,8,64,128]{3,2,1,0:T(8,128)} %copy-done.2, f32[4,16,8192]{2,1,0:T(8,128)} %get-tuple-element.90.refs_3_, ...), custom_call_target="tpu_custom_call", output_to_operand_aliasing={{0}: (3, {}), {1}: (4, {})} | custom-call | flops 5242880 | bytes 1572864 | tf_op jit(solution)/shard_map/final/pallas_call | solution.py:254
  171.0 14.0 %final.7 = (f32[4,16,8192]{2,1,0:T(8,128)}, f32[4,16,8192]{2,1,0:T(8,128)}) custom-call(s32[34]{0:T(128)} %pad_add_fusion.info.refs_0_, f32[1,8,64,128]{3,2,1,0:T(8,128)} %get-tuple-element.56.refs_1_, f32[1,8,64,128]{3,2,1,0:T(8,128)} %copy-done.3, f32[4,16,8192]{2,1,0:T(8,128)} %get-tuple-element.92.refs_3_, ...), custom_call_target="tpu_custom_call", output_to_operand_aliasing={{0}: (3, {}), {1}: (4, {})} | custom-call | flops 5242880 | bytes 1572864 | tf_op jit(solution)/shard_map/final/pallas_call | solution.py:254
  (63 shorter events, 8.3 us)
Async XLA Ops:
  5.7 19.2 %collective-permute-start.15 = (f32[1,8,64,128]{3,2,1,0:T(8,128)}, f32[1,8,64,128]{3,2,1,0:T(8,128)S(1)}, u32[]{:S(2)}, u32[]{:S(2)}) collective-permute-start(f32[1,8,64,128]{3,2,1,0:T(8,128)} %get-tuple-element.79), channel_id=1, source_target_pairs={{0,4},{4,0},{8,12},{12,8},{16,20},{20,16},{24,28},{28,24},{1,5},{5... | collective-permute-start | bytes 786440 | tf_op jit(solution)/shard_map/ppermute | solution.py:184
  13.2 18.3 %collective-permute-start.10 = (f32[1,8,64,128]{3,2,1,0:T(8,128)}, f32[1,8,64,128]{3,2,1,0:T(8,128)S(1)}, u32[]{:S(2)}, u32[]{:S(2)}) collective-permute-start(f32[1,8,64,128]{3,2,1,0:T(8,128)} %get-tuple-element.69), channel_id=1, source_target_pairs={{0,4},{4,0},{8,12},{12,8},{16,20},{20,16},{24,28},{28,24},{1,5},{5... | collective-permute-start | bytes 786440 | tf_op jit(solution)/shard_map/ppermute | solution.py:184
  17.7 6.5 %copy-start = (s32[4096]{0:T(1024)S(1)}, s32[4096]{0:T(1024)}, u32[]{:S(2)}) copy-start(s32[4096]{0:T(1024)} %spans.7) | copy-start | bytes 49156
  17.7 18.4 %collective-permute-start.5 = (f32[1,8,64,128]{3,2,1,0:T(8,128)}, f32[1,8,64,128]{3,2,1,0:T(8,128)S(1)}, u32[]{:S(2)}, u32[]{:S(2)}) collective-permute-start(f32[1,8,64,128]{3,2,1,0:T(8,128)} %get-tuple-element.59), channel_id=1, source_target_pairs={{0,4},{4,0},{8,12},{12,8},{16,20},{20,16},{24,28},{28,24},{1,5},{5... | collective-permute-start | bytes 786440 | tf_op jit(solution)/shard_map/ppermute | solution.py:184
  24.1 18.4 %collective-permute-start = (f32[1,8,64,128]{3,2,1,0:T(8,128)}, f32[1,8,64,128]{3,2,1,0:T(8,128)S(1)}, u32[]{:S(2)}, u32[]{:S(2)}) collective-permute-start(f32[1,8,64,128]{3,2,1,0:T(8,128)} %get-tuple-element.49), channel_id=1, source_target_pairs={{0,4},{4,0},{8,12},{12,8},{16,20},{20,16},{24,28},{28,24},{1,5},{5... | collective-permute-start | bytes 786440 | tf_op jit(solution)/shard_map/ppermute | solution.py:184
  24.9 0.7 copy-start.20
  29.4 17.7 %collective-permute-start.16 = (f32[1,8,64,128]{3,2,1,0:T(8,128)}, f32[1,8,64,128]{3,2,1,0:T(8,128)S(1)}, u32[]{:S(2)}, u32[]{:S(2)}) collective-permute-start(f32[1,8,64,128]{3,2,1,0:T(8,128)} %get-tuple-element.81), channel_id=1, source_target_pairs={{0,8},{4,12},{8,0},{12,4},{16,24},{20,28},{24,16},{28,20},{1,9},{5... | collective-permute-start | bytes 786440 | tf_op jit(solution)/shard_map/ppermute | solution.py:184
  31.5 0.7 copy-start.19
  36.0 18.6 %collective-permute-start.11 = (f32[1,8,64,128]{3,2,1,0:T(8,128)}, f32[1,8,64,128]{3,2,1,0:T(8,128)S(1)}, u32[]{:S(2)}, u32[]{:S(2)}) collective-permute-start(f32[1,8,64,128]{3,2,1,0:T(8,128)} %get-tuple-element.71), channel_id=1, source_target_pairs={{0,8},{4,12},{8,0},{12,4},{16,24},{20,28},{24,16},{28,20},{1,9},{5... | collective-permute-start | bytes 786440 | tf_op jit(solution)/shard_map/ppermute | solution.py:184
  36.1 0.7 copy-start.5
  40.5 18.6 %collective-permute-start.6 = (f32[1,8,64,128]{3,2,1,0:T(8,128)}, f32[1,8,64,128]{3,2,1,0:T(8,128)S(1)}, u32[]{:S(2)}, u32[]{:S(2)}) collective-permute-start(f32[1,8,64,128]{3,2,1,0:T(8,128)} %get-tuple-element.61), channel_id=1, source_target_pairs={{0,8},{4,12},{8,0},{12,4},{16,24},{20,28},{24,16},{28,20},{1,9},{5... | collective-permute-start | bytes 786440 | tf_op jit(solution)/shard_map/ppermute | solution.py:184
  42.6 0.7 copy-start.4
  47.0 19.5 %collective-permute-start.1 = (f32[1,8,64,128]{3,2,1,0:T(8,128)}, f32[1,8,64,128]{3,2,1,0:T(8,128)S(1)}, u32[]{:S(2)}, u32[]{:S(2)}) collective-permute-start(f32[1,8,64,128]{3,2,1,0:T(8,128)} %get-tuple-element.51), channel_id=1, source_target_pairs={{0,8},{4,12},{8,0},{12,4},{16,24},{20,28},{24,16},{28,20},{1,9},{5... | collective-permute-start | bytes 786440 | tf_op jit(solution)/shard_map/ppermute | solution.py:184
  47.1 0.7 copy-start.6
  51.5 31.9 %collective-permute-start.17 = (f32[1,8,64,128]{3,2,1,0:T(8,128)}, f32[1,8,64,128]{3,2,1,0:T(8,128)S(1)}, u32[]{:S(2)}, u32[]{:S(2)}) collective-permute-start(f32[1,8,64,128]{3,2,1,0:T(8,128)} %get-tuple-element.83), channel_id=1, source_target_pairs={{0,16},{4,20},{8,24},{12,28},{16,0},{20,4},{24,8},{28,12},{1,17},{... | collective-permute-start | bytes 786440 | tf_op jit(solution)/shard_map/ppermute | solution.py:184
  54.6 0.7 copy-start.7
  59.0 30.0 %collective-permute-start.12 = (f32[1,8,64,128]{3,2,1,0:T(8,128)}, f32[1,8,64,128]{3,2,1,0:T(8,128)S(1)}, u32[]{:S(2)}, u32[]{:S(2)}) collective-permute-start(f32[1,8,64,128]{3,2,1,0:T(8,128)} %get-tuple-element.73), channel_id=1, source_target_pairs={{0,16},{4,20},{8,24},{12,28},{16,0},{20,4},{24,8},{28,12},{1,17},{... | collective-permute-start | bytes 786440 | tf_op jit(solution)/shard_map/ppermute | solution.py:184
  59.1 0.7 copy-start.8
  63.5 31.1 %collective-permute-start.7 = (f32[1,8,64,128]{3,2,1,0:T(8,128)}, f32[1,8,64,128]{3,2,1,0:T(8,128)S(1)}, u32[]{:S(2)}, u32[]{:S(2)}) collective-permute-start(f32[1,8,64,128]{3,2,1,0:T(8,128)} %get-tuple-element.63), channel_id=1, source_target_pairs={{0,16},{4,20},{8,24},{12,28},{16,0},{20,4},{24,8},{28,12},{1,17},{... | collective-permute-start | bytes 786440 | tf_op jit(solution)/shard_map/ppermute | solution.py:184
  66.5 0.7 copy-start.9
  70.9 28.2 %collective-permute-start.2 = (f32[1,8,64,128]{3,2,1,0:T(8,128)}, f32[1,8,64,128]{3,2,1,0:T(8,128)S(1)}, u32[]{:S(2)}, u32[]{:S(2)}) collective-permute-start(f32[1,8,64,128]{3,2,1,0:T(8,128)} %get-tuple-element.53), channel_id=1, source_target_pairs={{0,16},{4,20},{8,24},{12,28},{16,0},{20,4},{24,8},{28,12},{1,17},{... | collective-permute-start | bytes 786440 | tf_op jit(solution)/shard_map/ppermute | solution.py:184
  83.4 0.7 copy-start.10
  87.8 16.3 %collective-permute-start.18 = (f32[1,8,64,128]{3,2,1,0:T(8,128)}, f32[1,8,64,128]{3,2,1,0:T(8,128)S(1)}, u32[]{:S(2)}, u32[]{:S(2)}) collective-permute-start(f32[1,8,64,128]{3,2,1,0:T(8,128)} %get-tuple-element.85), channel_id=1, source_target_pairs={{0,1},{1,0},{2,3},{3,2},{4,5},{5,4},{6,7},{7,6},{8,9},{9,8},{10,11... | collective-permute-start | bytes 786440 | tf_op jit(solution)/shard_map/ppermute | solution.py:184
  89.0 0.7 copy-start.11
  93.5 16.8 %collective-permute-start.13 = (f32[1,8,64,128]{3,2,1,0:T(8,128)}, f32[1,8,64,128]{3,2,1,0:T(8,128)S(1)}, u32[]{:S(2)}, u32[]{:S(2)}) collective-permute-start(f32[1,8,64,128]{3,2,1,0:T(8,128)} %get-tuple-element.75), channel_id=1, source_target_pairs={{0,1},{1,0},{2,3},{3,2},{4,5},{5,4},{6,7},{7,6},{8,9},{9,8},{10,11... | collective-permute-start | bytes 786440 | tf_op jit(solution)/shard_map/ppermute | solution.py:184
  94.6 0.7 copy-start.12
  99.1 16.1 %collective-permute-start.8 = (f32[1,8,64,128]{3,2,1,0:T(8,128)}, f32[1,8,64,128]{3,2,1,0:T(8,128)S(1)}, u32[]{:S(2)}, u32[]{:S(2)}) collective-permute-start(f32[1,8,64,128]{3,2,1,0:T(8,128)} %get-tuple-element.65), channel_id=1, source_target_pairs={{0,1},{1,0},{2,3},{3,2},{4,5},{5,4},{6,7},{7,6},{8,9},{9,8},{10,11... | collective-permute-start | bytes 786440 | tf_op jit(solution)/shard_map/ppermute | solution.py:184
  99.2 0.7 copy-start.13
  103.6 17.7 %collective-permute-start.3 = (f32[1,8,64,128]{3,2,1,0:T(8,128)}, f32[1,8,64,128]{3,2,1,0:T(8,128)S(1)}, u32[]{:S(2)}, u32[]{:S(2)}) collective-permute-start(f32[1,8,64,128]{3,2,1,0:T(8,128)} %get-tuple-element.55), channel_id=1, source_target_pairs={{0,1},{1,0},{2,3},{3,2},{4,5},{5,4},{6,7},{7,6},{8,9},{9,8},{10,11... | collective-permute-start | bytes 786440 | tf_op jit(solution)/shard_map/ppermute | solution.py:184
  104.2 0.7 copy-start.14
  108.6 17.6 %collective-permute-start.19 = (f32[1,8,64,128]{3,2,1,0:T(8,128)}, f32[1,8,64,128]{3,2,1,0:T(8,128)S(1)}, u32[]{:S(2)}, u32[]{:S(2)}) collective-permute-start(f32[1,8,64,128]{3,2,1,0:T(8,128)} %get-tuple-element.87), channel_id=1, source_target_pairs={{0,2},{1,3},{2,0},{3,1},{4,6},{5,7},{6,4},{7,5},{8,10},{9,11},{10,... | collective-permute-start | bytes 786440 | tf_op jit(solution)/shard_map/ppermute | solution.py:184
  110.3 0.7 copy-start.15
  114.7 26.1 %collective-permute-start.14 = (f32[1,8,64,128]{3,2,1,0:T(8,128)}, f32[1,8,64,128]{3,2,1,0:T(8,128)S(1)}, u32[]{:S(2)}, u32[]{:S(2)}) collective-permute-start(f32[1,8,64,128]{3,2,1,0:T(8,128)} %get-tuple-element.77), channel_id=1, source_target_pairs={{0,2},{1,3},{2,0},{3,1},{4,6},{5,7},{6,4},{7,5},{8,10},{9,11},{10,... | collective-permute-start | bytes 786440 | tf_op jit(solution)/shard_map/ppermute | solution.py:184
  115.2 0.7 copy-start.16
  119.6 35.9 %collective-permute-start.9 = (f32[1,8,64,128]{3,2,1,0:T(8,128)}, f32[1,8,64,128]{3,2,1,0:T(8,128)S(1)}, u32[]{:S(2)}, u32[]{:S(2)}) collective-permute-start(f32[1,8,64,128]{3,2,1,0:T(8,128)} %get-tuple-element.67), channel_id=1, source_target_pairs={{0,2},{1,3},{2,0},{3,1},{4,6},{5,7},{6,4},{7,5},{8,10},{9,11},{10,... | collective-permute-start | bytes 786440 | tf_op jit(solution)/shard_map/ppermute | solution.py:184
  121.4 0.7 copy-start.17
  125.8 44.5 %collective-permute-start.4 = (f32[1,8,64,128]{3,2,1,0:T(8,128)}, f32[1,8,64,128]{3,2,1,0:T(8,128)S(1)}, u32[]{:S(2)}, u32[]{:S(2)}) collective-permute-start(f32[1,8,64,128]{3,2,1,0:T(8,128)} %get-tuple-element.57), channel_id=1, source_target_pairs={{0,2},{1,3},{2,0},{3,1},{4,6},{5,7},{6,4},{7,5},{8,10},{9,11},{10,... | collective-permute-start | bytes 786440 | tf_op jit(solution)/shard_map/ppermute | solution.py:184
  126.2 0.7 copy-start.18
  140.9 0.7 copy-start.1
  155.6 0.7 copy-start.2
  170.2 0.7 copy-start.3
where the time goes:
time: 186 us; the launch traced here: 185 us
  Pallas kernels  133 us (72%)
  starting transfers between devices  20.7 us (11%)
  waiting for transfers between devices  14.7 us (8%)
  local copies, waits for them, and re-layouts  14 us (8%)
    pallas_call x16, Pallas kernels, merge(): pl.pallas_call(functools.partial(merge_kernel, step, tiles, pad), grid=(1...  59.5 us
    pallas_call x4, Pallas kernels, final(): pl.pallas_call(functools.partial(final_kernel, step, tiles, pad, 1.0 / ma...  55.8 us
    ppermute x20, starting transfers between devices, swapped(): lax.ppermute(value, axis, [(s, s ^ mask) for s in range(lax.axis_size(axi...  20.7 us
    pallas_call x4, Pallas kernels, local(): pl.pallas_call(functools.partial(local_kernel, chan_dev, tiles, pad), gri...  17.9 us
    ppermute x20, waiting for transfers between devices, swapped(): lax.ppermute(value, axis, [(s, s ^ mask) for s in range(lax.axis_size(axi...  14.7 us
    unnamed x42, local copies, waits for them, and re-layouts  14 us
  transfers between devices with their start and end apart: 20, of which 3 were waited for; matrix products, arithmetic and copies ran while one was open for 0% of the time, Pallas kernels for 62%

commit v1 on v0

v1 whole, which is shorter than its diff:
```python
import functools
import math

import jax
import jax.numpy as jnp
from jax import lax
from jax.experimental import pallas as pl
from jax.experimental.pallas import tpu as pltpu
from jax.sharding import PartitionSpec as P

ROWS_DEV = 16
BOXES = 9
LANES = 128
HALF = ROWS_DEV // 2


LANE_BITS = LANES.bit_length() - 1


def padding(longest_shift):
    return -(-(longest_shift // LANES + 1) // 8) * 8


def bit_of(number, position):
    return lax.shift_right_logical(number, jnp.int32(position)) & 1


def row_shifts(first_row, low, both, count):
    start = first_row * low
    shift = lax.div(start, both)
    rest = start - shift * both
    result = []
    for _ in range(count):
        result.append(shift)
        rest = rest + low
        over = rest >= both
        shift = jnp.where(over, shift + 1, shift)
        rest = jnp.where(over, rest - both, rest)
    return result


def delayed(source, lead, row, shift, pad, tiles):
    coarse = lax.shift_right_logical(shift, jnp.int32(LANE_BITS))
    fine = shift & (LANES - 1)
    here = source[lead, row, pl.ds(pad - coarse, tiles), :]
    before = source[lead, row, pl.ds(pad - coarse - 1, tiles), :]
    lane = lax.broadcasted_iota(jnp.int32, (tiles, LANES), 1)
    mixed = jnp.where(lane < LANES - fine, here, before)
    return pltpu.roll(mixed, fine, 1)


def local_kernel(beam, chan_dev, tiles, pad, parts, info, spans, sums, power, keep, send, *scratch):
    stage, wide, level_a, level_b, sems = scratch
    piece = tiles * LANES // parts
    copies = []
    for part in range(parts):
        columns = pl.ds(part * piece, piece)
        copies.append(
            pltpu.make_async_copy(
                power.at[beam, :, columns], stage.at[:, columns], sems.at[part]
            )
        )
        copies[-1].start()
    device = info[0]
    groups = HALF
    span = chan_dev // groups
    zero = jnp.zeros((pad, LANES), jnp.float32)
    for m in range(1, groups, 2):
        for r in range(1 if m > 1 else HALF):
            level_a[m, r, 0:pad, :] = zero
        for r in range(4):
            if m < 4:
                level_b[m, r, 0:pad, :] = zero
    widths = []
    for m in range(groups):
        total = spans[device * chan_dev + m * span]
        for c in range(1, span):
            total = total + spans[device * chan_dev + m * span + c]
        widths.append(total)
    for part in range(parts):
        copies[part].wait()
        value = jnp.dot(
            sums[...],
            stage[:, part * piece : (part + 1) * piece],
            preferred_element_type=jnp.float32,
        )
        for tile in range(piece // LANES):
            wide[part * (piece // LANES) + tile] = value[:, tile * LANES : (tile + 1) * LANES]
    for m in range(1, groups, 2):
        level_a[m, 0, pad : pad + tiles, :] = wide[:, m, :]
    source, target = level_a, level_b
    rows = 4
    bands = groups // 2
    old_rows = 1

    def low_row(m, q):
        if old_rows == 1:
            return wide[:, m, :]
        return source[m, q, pad : pad + tiles, :]

    while rows < ROWS_DEV:
        merged = []
        for m in range(bands):
            low, both = widths[2 * m], widths[2 * m] + widths[2 * m + 1]
            merged.append(both)
            shifts = row_shifts(jnp.int32(0), low, both, rows)
            for r in range(rows):
                q = r * old_rows // rows
                result = low_row(2 * m, q)
                if r < 2:
                    result = result + source[2 * m + 1, q, pad : pad + tiles, :]
                else:
                    result = result + delayed(source, 2 * m + 1, q, shifts[r], pad, tiles)
                target[m, r, pad : pad + tiles, :] = result
        widths = merged
        source, target = target, source
        old_rows, rows, bands = rows, rows * 2, bands // 2
    low, both = widths[0], widths[0] + widths[1]
    emit_halves(bit_of(device, 0), row_shifts(jnp.int32(0), low, both, ROWS_DEV), source, keep, send, pad, tiles)


def emit_halves(mine, shifts, held, keep, send, pad, tiles):
    for half, ref in ((1 - mine, send), (mine, keep)):
        for i in range(HALF):
            shift = jnp.where(half == 1, shifts[HALF + i], shifts[i])
            q = half * (HALF // 2) + i // 2
            ref[i] = held[0, q, pad : pad + tiles, :] + delayed(held, 1, q, shift, pad, tiles)


def fetch(step, tiles, pad, info, kept, came, held):
    device = info[0]
    mine = bit_of(device, step)
    zero = jnp.zeros((pad, LANES), jnp.float32)
    for q in range(HALF):
        held[1, q, 0:pad, :] = zero
    for q in range(HALF):
        held[mine, q, pad : pad + tiles, :] = kept[q]
        held[1 - mine, q, pad : pad + tiles, :] = came[q]
    block = jnp.int32(0)
    for position in range(step + 1):
        block = 2 * block + bit_of(device, position)
    size = 2**step
    first = lax.shift_right_logical(device, jnp.int32(step + 1)) * (2 * size)
    low = info[1 + first + size] - info[1 + first]
    both = info[1 + first + 2 * size] - info[1 + first]
    return row_shifts(block * ROWS_DEV, low, both, ROWS_DEV)


def merge_kernel(step, tiles, pad, info, kept, came, keep, send, held):
    shifts = fetch(step, tiles, pad, info, kept, came, held)
    emit_halves(bit_of(info[0], step + 1), shifts, held, keep, send, pad, tiles)


def final_kernel(beam, step, tiles, pad, scale, *refs):
    info, kept, came = refs[:3]
    plane, peak, held, run_a, run_b, best, out_plane, out_peak, sems = refs[-9:]
    shifts = fetch(step, tiles, pad, info, kept, came, held)
    lane = lax.broadcasted_iota(jnp.int32, (tiles, LANES), 1)
    zero = jnp.zeros((8, LANES), jnp.float32)
    copies = []
    for group in range(0, ROWS_DEV, 8):
        for i in range(8):
            r = group + i
            run_a[i, 0:8, :] = zero
            run_b[i, 0:8, :] = zero
            value = held[0, r // 2, pad : pad + tiles, :] + delayed(
                held, 1, r // 2, shifts[r], pad, tiles
            )
            value = value * scale
            run_a[i, 8 : 8 + tiles, :] = value
            best[i] = value
        for j in range(tiles):
            out_plane[group : group + 8, j * LANES : (j + 1) * LANES] = run_a[:, 8 + j, :]
        copies.append(
            pltpu.make_async_copy(
                out_plane.at[pl.ds(group, 8)], plane.at[beam, pl.ds(group, 8)], sems.at[0, group // 8]
            )
        )
        copies[-1].start()
        source, target = run_a, run_b
        width = 1
        for level in range(BOXES - 1):
            for i in range(8):
                here = source[i, 8 : 8 + tiles, :]
                before = source[i, 7 : 7 + tiles, :]
                if width < LANES:
                    moved = pltpu.roll(jnp.where(lane < LANES - width, here, before), width, 1)
                else:
                    moved = before
                value = here + moved
                target[i, 8 : 8 + tiles, :] = value
                best[i] = jnp.maximum(best[i], value * (1.0 / math.sqrt(2 * width)))
            source, target = target, source
            width = width * 2
        for j in range(tiles):
            out_peak[group : group + 8, j * LANES : (j + 1) * LANES] = best[:, j, :]
        copies.append(
            pltpu.make_async_copy(
                out_peak.at[pl.ds(group, 8)], peak.at[beam, pl.ds(group, 8)], sems.at[1, group // 8]
            )
        )
        copies[-1].start()
    for copy in copies:
        copy.wait()


SMEM = pl.BlockSpec(memory_space=pltpu.SMEM)
VMEM = pl.BlockSpec(memory_space=pltpu.VMEM)
HBM = pl.BlockSpec(memory_space=pltpu.HBM)


def swapped(value, axis, distance):
    mask = 2**distance
    return lax.ppermute(value, axis, [(s, s ^ mask) for s in range(lax.axis_size(axis))])


def on_device(intensity, channel_spans):
    beams, chan_dev, samples = intensity.shape
    sub_count = lax.axis_size("sub")
    band_size = lax.axis_size("band")
    devices = sub_count * band_size
    tiles = samples // LANES
    sub_bits = sub_count.bit_length() - 1
    bits = devices.bit_length() - 1
    device = lax.axis_index("band") * sub_count + lax.axis_index("sub")
    totals = channel_spans.reshape(devices, chan_dev).sum(axis=1)
    edge = jnp.arange(devices + 1)[:, None] > jnp.arange(devices)[None, :]
    edges = jnp.where(edge, totals[None, :], 0).sum(axis=1)
    info = jnp.concatenate([device.reshape(1), edges]).astype(jnp.int32)
    place = device.reshape(1).astype(jnp.int32)
    group = jnp.arange(chan_dev) // (chan_dev // HALF)
    sums = (jnp.arange(HALF)[:, None] == group[None, :]).astype(jnp.bfloat16)
    halves = jax.ShapeDtypeStruct((HALF, tiles, LANES), jnp.float32)
    whole = jax.ShapeDtypeStruct((beams, ROWS_DEV, samples), jnp.float32)
    size = HALF * tiles * LANES
    parts = 4

    def local(beam):
        pad = padding(ROWS_DEV)
        padded = pltpu.VMEM((HALF, HALF, pad + tiles, LANES), jnp.float32)
        return pl.pallas_call(
            functools.partial(local_kernel, beam, chan_dev, tiles, pad, parts),
            in_specs=[SMEM, SMEM, VMEM, HBM],
            out_specs=[VMEM, VMEM],
            out_shape=[halves, halves],
            scratch_shapes=[
                pltpu.VMEM((chan_dev, samples), jnp.bfloat16),
                pltpu.VMEM((tiles, HALF, LANES), jnp.float32),
                padded,
                padded,
                pltpu.SemaphoreType.DMA((parts,)),
            ],
            compiler_params=pltpu.CompilerParams(vmem_limit_bytes=12 << 20),
            cost_estimate=pl.CostEstimate(
                flops=size * 40, bytes_accessed=chan_dev * samples * 2 + size * 8, transcendentals=0
            ),
            name="local",
        )(place, channel_spans, sums, intensity)

    def merge(step, kept, came):
        pad = padding(ROWS_DEV * 2 ** (step + 1))
        return pl.pallas_call(
            functools.partial(merge_kernel, step, tiles, pad),
            in_specs=[SMEM, VMEM, VMEM],
            out_specs=[VMEM, VMEM],
            out_shape=[halves, halves],
            scratch_shapes=[pltpu.VMEM((2, HALF, pad + tiles, LANES), jnp.float32)],
            compiler_params=pltpu.CompilerParams(vmem_limit_bytes=4 << 20),
            cost_estimate=pl.CostEstimate(
                flops=size * 8, bytes_accessed=size * 16, transcendentals=0
            ),
            name=f"merge{step}",
        )(info, kept, came)

    def final(beam, kept, came, done):
        step = bits - 1
        pad = padding(ROWS_DEV * 2**bits)
        run = pltpu.VMEM((8, 8 + tiles, LANES), jnp.float32)
        rows = pltpu.VMEM((ROWS_DEV, samples), jnp.float32)
        return pl.pallas_call(
            functools.partial(
                final_kernel, beam, step, tiles, pad, 1.0 / math.sqrt(chan_dev * devices)
            ),
            in_specs=[SMEM, VMEM, VMEM] + [HBM] * len(done),
            out_specs=[HBM, HBM],
            out_shape=[whole, whole],
            scratch_shapes=[
                pltpu.VMEM((2, HALF, pad + tiles, LANES), jnp.float32),
                run,
                run,
                pltpu.VMEM((8, tiles, LANES), jnp.float32),
                rows,
                rows,
                pltpu.SemaphoreType.DMA((2, ROWS_DEV // 8)),
            ],
            input_output_aliases={3 + i: i for i in range(len(done))},
            compiler_params=pltpu.CompilerParams(vmem_limit_bytes=12 << 20),
            cost_estimate=pl.CostEstimate(
                flops=size * 80, bytes_accessed=size * 24, transcendentals=0
            ),
            name="final",
        )(info, kept, came, *done)

    state = [local(beam) for beam in range(beams)]
    for step in range(bits):
        axis, distance = ("sub", step) if step < sub_bits else ("band", step - sub_bits)
        came = [swapped(send, axis, distance) for _, send in state]
        if step < bits - 1:
            state = [merge(step, state[b][0], came[b]) for b in range(beams)]
    done = ()
    for beam in range(beams):
        done = final(beam, state[beam][0], came[beam], done)
    return tuple(done)


def solution(mesh):
    spec = P(None, ("band", "sub"), None)
    return jax.shard_map(
        on_device, mesh=mesh, in_specs=(spec, P()), out_specs=(spec, spec), check_vma=False
    )
```

time: 186 us -> 116 us (0.62)
  Pallas kernels: 133 us -> 37.4 us
  waiting for transfers between devices: 14.7 us -> 49.6 us
  local copies, waits for them, and re-layouts: 14 us -> 4.09 us
  starting transfers between devices: 20.7 us -> 22.8 us
    pallas_call x24, Pallas kernels: 133 us -> 37.4 us  [the longest x4 14.5 us: final(): pl.pallas_call(functools.partial(final_kernel, beam, step, tiles, pad, 1....]
    ppermute x20, waiting for transfers between devices: 14.7 us -> 49.6 us  [swapped(): lax.ppermute(value, axis, [(s, s ^ mask) for s in range(lax.axis_size(axi...]
    unnamed x42 -> x4, local copies, waits for them, and re-layouts: 14 us -> 4.09 us
    ppermute x20, starting transfers between devices: 20.7 us -> 22.8 us  [swapped(): lax.ppermute(value, axis, [(s, s ^ mask) for s in range(lax.axis_size(axi...]
  transfers between devices with their start and end apart: 20 -> 20, of which waited for: 3 -> 11; matrix products, arithmetic and copies ran while one was open for 0% -> 0% of each run, Pallas kernels for 62% -> 27%
where the time goes in v1:
time: 116 us; the launch traced here: 115 us
  waiting for transfers between devices  49.6 us (43%)
  Pallas kernels  37.4 us (32%)
  starting transfers between devices  22.8 us (20%)
  local copies, waits for them, and re-layouts  4.09 us (4%)
    ppermute x20, waiting for transfers between devices, swapped(): lax.ppermute(value, axis, [(s, s ^ mask) for s in range(lax.axis_size(axi...  49.6 us
    ppermute x20, starting transfers between devices, swapped(): lax.ppermute(value, axis, [(s, s ^ mask) for s in range(lax.axis_size(axi...  22.8 us
    pallas_call x4, Pallas kernels, final(): pl.pallas_call(functools.partial(final_kernel, beam, step, tiles, pad, 1....  14.5 us
    pallas_call x16, Pallas kernels, merge(): pl.pallas_call(functools.partial(merge_kernel, step, tiles, pad), in_spec...  13 us
    pallas_call x4, Pallas kernels, local(): pl.pallas_call(functools.partial(local_kernel, beam, chan_dev, tiles, pad...  9.96 us
    unnamed x4, local copies, waits for them, and re-layouts  4.09 us
  transfers between devices with their start and end apart: 20, of which 11 were waited for; matrix products, arithmetic and copies ran while one was open for 0% of the time, Pallas kernels for 27%

profile of v1, /device:TPU:0, one launch (start us, length us, event | category | flops | bytes accessed | tf_op | source)
XLA Modules:
  0.0 115.3 jit_solution(1132789630406556418)
XLA Ops:
  0.7 3.4 %copy-done = bf16[4,128,8192]{2,1,0:T(8,128)(2,1)S(1)} copy-done((bf16[4,128,8192]{2,1,0:T(8,128)(2,1)S(1)}, bf16[4,128,8192]{2,1,0:T(8,128)(2,1)}, u32[]{:S(2)}) %copy-start) | copy-done | bytes 8388632
  4.1 0.7 copy-done.1
  4.8 2.4 %local.7 = (f32[8,64,128]{2,1,0:T(8,128)S(1)}, f32[8,64,128]{2,1,0:T(8,128)S(1)}) custom-call(s32[1]{0:T(128)} %bitcast.info, s32[4096]{0:T(1024)S(1)} %copy-done.1, bf16[8,128]{1,0:T(8,128)(2,1)S(1)} %fusion.sums, bf16[4,128,8192]{2,1,0:T(8,128)(2,1)S(1)} %copy-done), custom_call_target="tpu_custom_call" | custom-call | flops 2621440 | bytes 2621440 | tf_op jit(solution)/shard_map/local/pallas_call | solution.py:241
  7.2 3.1 %collective-permute-start.15 = (f32[8,64,128]{2,1,0:T(8,128)S(1)}, f32[8,64,128]{2,1,0:T(8,128)S(1)}, u32[]{:S(2)}, u32[]{:S(2)}) collective-permute-start(f32[8,64,128]{2,1,0:T(8,128)S(1)} %get-tuple-element.79), channel_id=1, source_target_pairs={{0,4},{4,0},{8,12},{12,8},{16,20},{20,16},{24,28},{28,24},{1,5},{5... | collective-permute-start | bytes 786440 | tf_op jit(solution)/shard_map/ppermute | solution.py:214
  10.3 2.4 %local.6 = (f32[8,64,128]{2,1,0:T(8,128)S(1)}, f32[8,64,128]{2,1,0:T(8,128)S(1)}) custom-call(s32[1]{0:T(128)} %bitcast.info, s32[4096]{0:T(1024)S(1)} %copy-done.1, bf16[8,128]{1,0:T(8,128)(2,1)S(1)} %fusion.sums, bf16[4,128,8192]{2,1,0:T(8,128)(2,1)S(1)} %copy-done), custom_call_target="tpu_custom_call" | custom-call | flops 2621440 | bytes 2621440 | tf_op jit(solution)/shard_map/local/pallas_call | solution.py:241
  12.8 2.4 %local.5 = (f32[8,64,128]{2,1,0:T(8,128)S(1)}, f32[8,64,128]{2,1,0:T(8,128)S(1)}) custom-call(s32[1]{0:T(128)} %bitcast.info, s32[4096]{0:T(1024)S(1)} %copy-done.1, bf16[8,128]{1,0:T(8,128)(2,1)S(1)} %fusion.sums, bf16[4,128,8192]{2,1,0:T(8,128)(2,1)S(1)} %copy-done), custom_call_target="tpu_custom_call" | custom-call | flops 2621440 | bytes 2621440 | tf_op jit(solution)/shard_map/local/pallas_call | solution.py:241
  15.3 2.1 %collective-permute-start.5 = (f32[8,64,128]{2,1,0:T(8,128)S(1)}, f32[8,64,128]{2,1,0:T(8,128)S(1)}, u32[]{:S(2)}, u32[]{:S(2)}) collective-permute-start(f32[8,64,128]{2,1,0:T(8,128)S(1)} %get-tuple-element.59), channel_id=1, source_target_pairs={{0,4},{4,0},{8,12},{12,8},{16,20},{20,16},{24,28},{28,24},{1,5},{5... | collective-permute-start | bytes 786440 | tf_op jit(solution)/shard_map/ppermute | solution.py:214
  17.3 2.6 %local.4 = (f32[8,64,128]{2,1,0:T(8,128)S(1)}, f32[8,64,128]{2,1,0:T(8,128)S(1)}) custom-call(s32[1]{0:T(128)} %bitcast.info, s32[4096]{0:T(1024)S(1)} %copy-done.1, bf16[8,128]{1,0:T(8,128)(2,1)S(1)} %fusion.sums, bf16[4,128,8192]{2,1,0:T(8,128)(2,1)S(1)} %copy-done), custom_call_target="tpu_custom_call" | custom-call | flops 2621440 | bytes 2621440 | tf_op jit(solution)/shard_map/local/pallas_call | solution.py:241
  20.3 0.8 merge0.7
  21.2 2.1 %collective-permute-start.16 = (f32[8,64,128]{2,1,0:T(8,128)S(1)}, f32[8,64,128]{2,1,0:T(8,128)S(1)}, u32[]{:S(2)}, u32[]{:S(2)}) collective-permute-start(f32[8,64,128]{2,1,0:T(8,128)S(1)} %get-tuple-element.81), channel_id=1, source_target_pairs={{0,8},{4,12},{8,0},{12,4},{16,24},{20,28},{24,16},{28,20},{1,9},{5... | collective-permute-start | bytes 786440 | tf_op jit(solution)/shard_map/ppermute | solution.py:214
  23.3 0.8 merge0.6
  24.1 1.9 %collective-permute-start.11 = (f32[8,64,128]{2,1,0:T(8,128)S(1)}, f32[8,64,128]{2,1,0:T(8,128)S(1)}, u32[]{:S(2)}, u32[]{:S(2)}) collective-permute-start(f32[8,64,128]{2,1,0:T(8,128)S(1)} %get-tuple-element.71), channel_id=1, source_target_pairs={{0,8},{4,12},{8,0},{12,4},{16,24},{20,28},{24,16},{28,20},{1,9},{5... | collective-permute-start | bytes 786440 | tf_op jit(solution)/shard_map/ppermute | solution.py:214
  26.0 2.7 %collective-permute-done.5.came = f32[8,64,128]{2,1,0:T(8,128)S(1)} collective-permute-done((f32[8,64,128]{2,1,0:T(8,128)S(1)}, f32[8,64,128]{2,1,0:T(8,128)S(1)}, u32[]{:S(2)}, u32[]{:S(2)}) %collective-permute-start.5) | collective-permute-done | bytes 262176 | tf_op jit(solution)/shard_map/ppermute | solution.py:214
  28.7 0.8 merge0.5
  29.5 2.1 %collective-permute-start.6 = (f32[8,64,128]{2,1,0:T(8,128)S(1)}, f32[8,64,128]{2,1,0:T(8,128)S(1)}, u32[]{:S(2)}, u32[]{:S(2)}) collective-permute-start(f32[8,64,128]{2,1,0:T(8,128)S(1)} %get-tuple-element.61), channel_id=1, source_target_pairs={{0,8},{4,12},{8,0},{12,4},{16,24},{20,28},{24,16},{28,20},{1,9},{5... | collective-permute-start | bytes 786440 | tf_op jit(solution)/shard_map/ppermute | solution.py:214
  31.6 1.8 %collective-permute-done.came = f32[8,64,128]{2,1,0:T(8,128)S(1)} collective-permute-done((f32[8,64,128]{2,1,0:T(8,128)S(1)}, f32[8,64,128]{2,1,0:T(8,128)S(1)}, u32[]{:S(2)}, u32[]{:S(2)}) %collective-permute-start) | collective-permute-done | bytes 262176 | tf_op jit(solution)/shard_map/ppermute | solution.py:214
  33.4 0.8 merge0.4
  34.3 1.9 %collective-permute-start.1 = (f32[8,64,128]{2,1,0:T(8,128)S(1)}, f32[8,64,128]{2,1,0:T(8,128)S(1)}, u32[]{:S(2)}, u32[]{:S(2)}) collective-permute-start(f32[8,64,128]{2,1,0:T(8,128)S(1)} %get-tuple-element.51), channel_id=1, source_target_pairs={{0,8},{4,12},{8,0},{12,4},{16,24},{20,28},{24,16},{28,20},{1,9},{5... | collective-permute-start | bytes 786440 | tf_op jit(solution)/shard_map/ppermute | solution.py:214
  36.1 0.8 merge1.7
  36.9 2.7 %collective-permute-start.17 = (f32[8,64,128]{2,1,0:T(8,128)S(1)}, f32[8,64,128]{2,1,0:T(8,128)S(1)}, u32[]{:S(2)}, u32[]{:S(2)}) collective-permute-start(f32[8,64,128]{2,1,0:T(8,128)S(1)} %get-tuple-element.83), channel_id=1, source_target_pairs={{0,16},{4,20},{8,24},{12,28},{16,0},{20,4},{24,8},{28,12},{1,17},{... | collective-permute-start | bytes 786440 | tf_op jit(solution)/shard_map/ppermute | solution.py:214
  39.6 0.8 merge1.6
  40.8 9.3 %collective-permute-done.6.came = f32[8,64,128]{2,1,0:T(8,128)S(1)} collective-permute-done((f32[8,64,128]{2,1,0:T(8,128)S(1)}, f32[8,64,128]{2,1,0:T(8,128)S(1)}, u32[]{:S(2)}, u32[]{:S(2)}) %collective-permute-start.6) | collective-permute-done | bytes 262176 | tf_op jit(solution)/shard_map/ppermute | solution.py:214
  50.1 0.8 merge1.5
  50.9 1.1 collective-permute-start.7
  52.0 1.8 %collective-permute-done.1.came = f32[8,64,128]{2,1,0:T(8,128)S(1)} collective-permute-done((f32[8,64,128]{2,1,0:T(8,128)S(1)}, f32[8,64,128]{2,1,0:T(8,128)S(1)}, u32[]{:S(2)}, u32[]{:S(2)}) %collective-permute-start.1) | collective-permute-done | bytes 262176 | tf_op jit(solution)/shard_map/ppermute | solution.py:214
  53.7 0.8 merge1.4
  54.5 0.8 collective-permute-start.2
  55.3 0.8 merge2.7
  56.2 18.9 %collective-permute-done.12.came = f32[8,64,128]{2,1,0:T(8,128)S(1)} collective-permute-done((f32[8,64,128]{2,1,0:T(8,128)S(1)}, f32[8,64,128]{2,1,0:T(8,128)S(1)}, u32[]{:S(2)}, u32[]{:S(2)}) %collective-permute-start.12) | collective-permute-done | bytes 262176 | tf_op jit(solution)/shard_map/ppermute | solution.py:214
  75.2 0.8 merge2.6
  76.1 4.7 %collective-permute-done.7.came = f32[8,64,128]{2,1,0:T(8,128)S(1)} collective-permute-done((f32[8,64,128]{2,1,0:T(8,128)S(1)}, f32[8,64,128]{2,1,0:T(8,128)S(1)}, u32[]{:S(2)}, u32[]{:S(2)}) %collective-permute-start.7) | collective-permute-done | bytes 262176 | tf_op jit(solution)/shard_map/ppermute | solution.py:214
  80.8 0.8 merge2.5
  81.7 2.5 %collective-permute-done.2.came = f32[8,64,128]{2,1,0:T(8,128)S(1)} collective-permute-done((f32[8,64,128]{2,1,0:T(8,128)S(1)}, f32[8,64,128]{2,1,0:T(8,128)S(1)}, u32[]{:S(2)}, u32[]{:S(2)}) %collective-permute-start.2) | collective-permute-done | bytes 262176 | tf_op jit(solution)/shard_map/ppermute | solution.py:214
  84.2 0.8 merge2.4
  85.1 0.8 merge3.7
  85.9 1.6 %collective-permute-start.19 = (f32[8,64,128]{2,1,0:T(8,128)S(1)}, f32[8,64,128]{2,1,0:T(8,128)S(1)}, u32[]{:S(2)}, u32[]{:S(2)}) collective-permute-start(f32[8,64,128]{2,1,0:T(8,128)S(1)} %get-tuple-element.87), channel_id=1, source_target_pairs={{0,2},{1,3},{2,0},{3,1},{4,6},{5,7},{6,4},{7,5},{8,10},{9,11},{10,... | collective-permute-start | bytes 786440 | tf_op jit(solution)/shard_map/ppermute | solution.py:214
  87.5 0.8 merge3.6
  88.9 0.8 merge3.5
  89.7 1.6 %collective-permute-start.9 = (f32[8,64,128]{2,1,0:T(8,128)S(1)}, f32[8,64,128]{2,1,0:T(8,128)S(1)}, u32[]{:S(2)}, u32[]{:S(2)}) collective-permute-start(f32[8,64,128]{2,1,0:T(8,128)S(1)} %get-tuple-element.67), channel_id=1, source_target_pairs={{0,2},{1,3},{2,0},{3,1},{4,6},{5,7},{6,4},{7,5},{8,10},{9,11},{10,... | collective-permute-start | bytes 786440 | tf_op jit(solution)/shard_map/ppermute | solution.py:214
  91.3 0.8 merge3.4
  92.7 2.5 %collective-permute-done.19.refs_2_ = f32[8,64,128]{2,1,0:T(8,128)S(1)} collective-permute-done((f32[8,64,128]{2,1,0:T(8,128)S(1)}, f32[8,64,128]{2,1,0:T(8,128)S(1)}, u32[]{:S(2)}, u32[]{:S(2)}) %collective-permute-start.19) | collective-permute-done | bytes 262176 | tf_op jit(solution)/shard_map/ppermute | solution.py:214
  95.2 3.6 %final.4 = (f32[4,16,8192]{2,1,0:T(8,128)}, f32[4,16,8192]{2,1,0:T(8,128)}) custom-call(s32[34]{0:T(128)S(1)} %pad_add_fusion.info.refs_0_, f32[8,64,128]{2,1,0:T(8,128)S(1)} %get-tuple-element.86.refs_1_, f32[8,64,128]{2,1,0:T(8,128)S(1)} %collective-permute-done.19.refs_2_), custom_call_target="tpu_custom_call" | custom-call | flops 5242880 | bytes 1572864 | tf_op jit(solution)/shard_map/final/pallas_call | solution.py:280
  98.7 2.0 %collective-permute-done.14.refs_2_ = f32[8,64,128]{2,1,0:T(8,128)S(1)} collective-permute-done((f32[8,64,128]{2,1,0:T(8,128)S(1)}, f32[8,64,128]{2,1,0:T(8,128)S(1)}, u32[]{:S(2)}, u32[]{:S(2)}) %collective-permute-start.14) | collective-permute-done | bytes 262176 | tf_op jit(solution)/shard_map/ppermute | solution.py:214
  100.8 3.6 %final.5 = (f32[4,16,8192]{2,1,0:T(8,128)}, f32[4,16,8192]{2,1,0:T(8,128)}) custom-call(s32[34]{0:T(128)S(1)} %pad_add_fusion.info.refs_0_, f32[8,64,128]{2,1,0:T(8,128)S(1)} %get-tuple-element.76.refs_1_, f32[8,64,128]{2,1,0:T(8,128)S(1)} %collective-permute-done.14.refs_2_, ...), custom_call_target="tpu_custom_call", output_to_operand_aliasing={{0}: (3, {}), {1}: (4, {})} | custom-call | flops 5242880 | bytes 1572864 | tf_op jit(solution)/shard_map/final/pallas_call | solution.py:280
  104.4 2.0 %collective-permute-done.9.refs_2_ = f32[8,64,128]{2,1,0:T(8,128)S(1)} collective-permute-done((f32[8,64,128]{2,1,0:T(8,128)S(1)}, f32[8,64,128]{2,1,0:T(8,128)S(1)}, u32[]{:S(2)}, u32[]{:S(2)}) %collective-permute-start.9) | collective-permute-done | bytes 262176 | tf_op jit(solution)/shard_map/ppermute | solution.py:214
  106.4 3.8 %final.6 = (f32[4,16,8192]{2,1,0:T(8,128)}, f32[4,16,8192]{2,1,0:T(8,128)}) custom-call(s32[34]{0:T(128)S(1)} %pad_add_fusion.info.refs_0_, f32[8,64,128]{2,1,0:T(8,128)S(1)} %get-tuple-element.66.refs_1_, f32[8,64,128]{2,1,0:T(8,128)S(1)} %collective-permute-done.9.refs_2_, ...), custom_call_target="tpu_custom_call", output_to_operand_aliasing={{0}: (3, {}), {1}: (4, {})} | custom-call | flops 5242880 | bytes 1572864 | tf_op jit(solution)/shard_map/final/pallas_call | solution.py:280
  110.2 1.3 %collective-permute-done.4.refs_2_ = f32[8,64,128]{2,1,0:T(8,128)S(1)} collective-permute-done((f32[8,64,128]{2,1,0:T(8,128)S(1)}, f32[8,64,128]{2,1,0:T(8,128)S(1)}, u32[]{:S(2)}, u32[]{:S(2)}) %collective-permute-start.4) | collective-permute-done | bytes 262176 | tf_op jit(solution)/shard_map/ppermute | solution.py:214
  111.5 3.6 %final.7 = (f32[4,16,8192]{2,1,0:T(8,128)}, f32[4,16,8192]{2,1,0:T(8,128)}) custom-call(s32[34]{0:T(128)S(1)} %pad_add_fusion.info.refs_0_, f32[8,64,128]{2,1,0:T(8,128)S(1)} %get-tuple-element.56.refs_1_, f32[8,64,128]{2,1,0:T(8,128)S(1)} %collective-permute-done.4.refs_2_, ...), custom_call_target="tpu_custom_call", output_to_operand_aliasing={{0}: (3, {}), {1}: (4, {})} | custom-call | flops 5242880 | bytes 1572864 | tf_op jit(solution)/shard_map/final/pallas_call | solution.py:280
  (25 shorter events, 2.4 us)
Async XLA Ops:
  0.7 3.4 %copy-start = (bf16[4,128,8192]{2,1,0:T(8,128)(2,1)S(1)}, bf16[4,128,8192]{2,1,0:T(8,128)(2,1)}, u32[]{:S(2)}) copy-start(bf16[4,128,8192]{2,1,0:T(8,128)(2,1)} %power.7) | copy-start | bytes 25165828
  4.1 0.7 copy-start.1
  7.2 13.1 %collective-permute-start.15 = (f32[8,64,128]{2,1,0:T(8,128)S(1)}, f32[8,64,128]{2,1,0:T(8,128)S(1)}, u32[]{:S(2)}, u32[]{:S(2)}) collective-permute-start(f32[8,64,128]{2,1,0:T(8,128)S(1)} %get-tuple-element.79), channel_id=1, source_target_pairs={{0,4},{4,0},{8,12},{12,8},{16,20},{20,16},{24,28},{28,24},{1,5},{5... | collective-permute-start | bytes 786440 | tf_op jit(solution)/shard_map/ppermute | solution.py:214
  12.7 10.6 %collective-permute-start.10 = (f32[8,64,128]{2,1,0:T(8,128)S(1)}, f32[8,64,128]{2,1,0:T(8,128)S(1)}, u32[]{:S(2)}, u32[]{:S(2)}) collective-permute-start(f32[8,64,128]{2,1,0:T(8,128)S(1)} %get-tuple-element.69), channel_id=1, source_target_pairs={{0,4},{4,0},{8,12},{12,8},{16,20},{20,16},{24,28},{28,24},{1,5},{5... | collective-permute-start | bytes 786440 | tf_op jit(solution)/shard_map/ppermute | solution.py:214
  15.3 13.4 %collective-permute-start.5 = (f32[8,64,128]{2,1,0:T(8,128)S(1)}, f32[8,64,128]{2,1,0:T(8,128)S(1)}, u32[]{:S(2)}, u32[]{:S(2)}) collective-permute-start(f32[8,64,128]{2,1,0:T(8,128)S(1)} %get-tuple-element.59), channel_id=1, source_target_pairs={{0,4},{4,0},{8,12},{12,8},{16,20},{20,16},{24,28},{28,24},{1,5},{5... | collective-permute-start | bytes 786440 | tf_op jit(solution)/shard_map/ppermute | solution.py:214
  20.0 13.5 %collective-permute-start = (f32[8,64,128]{2,1,0:T(8,128)S(1)}, f32[8,64,128]{2,1,0:T(8,128)S(1)}, u32[]{:S(2)}, u32[]{:S(2)}) collective-permute-start(f32[8,64,128]{2,1,0:T(8,128)S(1)} %get-tuple-element.49), channel_id=1, source_target_pairs={{0,4},{4,0},{8,12},{12,8},{16,20},{20,16},{24,28},{28,24},{1,5},{5... | collective-permute-start | bytes 786440 | tf_op jit(solution)/shard_map/ppermute | solution.py:214
  21.2 15.0 %collective-permute-start.16 = (f32[8,64,128]{2,1,0:T(8,128)S(1)}, f32[8,64,128]{2,1,0:T(8,128)S(1)}, u32[]{:S(2)}, u32[]{:S(2)}) collective-permute-start(f32[8,64,128]{2,1,0:T(8,128)S(1)} %get-tuple-element.81), channel_id=1, source_target_pairs={{0,8},{4,12},{8,0},{12,4},{16,24},{20,28},{24,16},{28,20},{1,9},{5... | collective-permute-start | bytes 786440 | tf_op jit(solution)/shard_map/ppermute | solution.py:214
  24.1 15.5 %collective-permute-start.11 = (f32[8,64,128]{2,1,0:T(8,128)S(1)}, f32[8,64,128]{2,1,0:T(8,128)S(1)}, u32[]{:S(2)}, u32[]{:S(2)}) collective-permute-start(f32[8,64,128]{2,1,0:T(8,128)S(1)} %get-tuple-element.71), channel_id=1, source_target_pairs={{0,8},{4,12},{8,0},{12,4},{16,24},{20,28},{24,16},{28,20},{1,9},{5... | collective-permute-start | bytes 786440 | tf_op jit(solution)/shard_map/ppermute | solution.py:214
  29.5 20.6 %collective-permute-start.6 = (f32[8,64,128]{2,1,0:T(8,128)S(1)}, f32[8,64,128]{2,1,0:T(8,128)S(1)}, u32[]{:S(2)}, u32[]{:S(2)}) collective-permute-start(f32[8,64,128]{2,1,0:T(8,128)S(1)} %get-tuple-element.61), channel_id=1, source_target_pairs={{0,8},{4,12},{8,0},{12,4},{16,24},{20,28},{24,16},{28,20},{1,9},{5... | collective-permute-start | bytes 786440 | tf_op jit(solution)/shard_map/ppermute | solution.py:214
  34.3 19.5 %collective-permute-start.1 = (f32[8,64,128]{2,1,0:T(8,128)S(1)}, f32[8,64,128]{2,1,0:T(8,128)S(1)}, u32[]{:S(2)}, u32[]{:S(2)}) collective-permute-start(f32[8,64,128]{2,1,0:T(8,128)S(1)} %get-tuple-element.51), channel_id=1, source_target_pairs={{0,8},{4,12},{8,0},{12,4},{16,24},{20,28},{24,16},{28,20},{1,9},{5... | collective-permute-start | bytes 786440 | tf_op jit(solution)/shard_map/ppermute | solution.py:214
  36.9 18.4 %collective-permute-start.17 = (f32[8,64,128]{2,1,0:T(8,128)S(1)}, f32[8,64,128]{2,1,0:T(8,128)S(1)}, u32[]{:S(2)}, u32[]{:S(2)}) collective-permute-start(f32[8,64,128]{2,1,0:T(8,128)S(1)} %get-tuple-element.83), channel_id=1, source_target_pairs={{0,16},{4,20},{8,24},{12,28},{16,0},{20,4},{24,8},{28,12},{1,17},{... | collective-permute-start | bytes 786440 | tf_op jit(solution)/shard_map/ppermute | solution.py:214
  40.4 34.8 %collective-permute-start.12 = (f32[8,64,128]{2,1,0:T(8,128)S(1)}, f32[8,64,128]{2,1,0:T(8,128)S(1)}, u32[]{:S(2)}, u32[]{:S(2)}) collective-permute-start(f32[8,64,128]{2,1,0:T(8,128)S(1)} %get-tuple-element.73), channel_id=1, source_target_pairs={{0,16},{4,20},{8,24},{12,28},{16,0},{20,4},{24,8},{28,12},{1,17},{... | collective-permute-start | bytes 786440 | tf_op jit(solution)/shard_map/ppermute | solution.py:214
  50.9 29.9 %collective-permute-start.7 = (f32[8,64,128]{2,1,0:T(8,128)S(1)}, f32[8,64,128]{2,1,0:T(8,128)S(1)}, u32[]{:S(2)}, u32[]{:S(2)}) collective-permute-start(f32[8,64,128]{2,1,0:T(8,128)S(1)} %get-tuple-element.63), channel_id=1, source_target_pairs={{0,16},{4,20},{8,24},{12,28},{16,0},{20,4},{24,8},{28,12},{1,17},{... | collective-permute-start | bytes 786440 | tf_op jit(solution)/shard_map/ppermute | solution.py:214
  54.5 29.6 %collective-permute-start.2 = (f32[8,64,128]{2,1,0:T(8,128)S(1)}, f32[8,64,128]{2,1,0:T(8,128)S(1)}, u32[]{:S(2)}, u32[]{:S(2)}) collective-permute-start(f32[8,64,128]{2,1,0:T(8,128)S(1)} %get-tuple-element.53), channel_id=1, source_target_pairs={{0,16},{4,20},{8,24},{12,28},{16,0},{20,4},{24,8},{28,12},{1,17},{... | collective-permute-start | bytes 786440 | tf_op jit(solution)/shard_map/ppermute | solution.py:214
  56.1 28.9 %collective-permute-start.18 = (f32[8,64,128]{2,1,0:T(8,128)S(1)}, f32[8,64,128]{2,1,0:T(8,128)S(1)}, u32[]{:S(2)}, u32[]{:S(2)}) collective-permute-start(f32[8,64,128]{2,1,0:T(8,128)S(1)} %get-tuple-element.85), channel_id=1, source_target_pairs={{0,1},{1,0},{2,3},{3,2},{4,5},{5,4},{6,7},{7,6},{8,9},{9,8},{10,11... | collective-permute-start | bytes 786440 | tf_op jit(solution)/shard_map/ppermute | solution.py:214
  76.0 11.5 %collective-permute-start.13 = (f32[8,64,128]{2,1,0:T(8,128)S(1)}, f32[8,64,128]{2,1,0:T(8,128)S(1)}, u32[]{:S(2)}, u32[]{:S(2)}) collective-permute-start(f32[8,64,128]{2,1,0:T(8,128)S(1)} %get-tuple-element.75), channel_id=1, source_target_pairs={{0,1},{1,0},{2,3},{3,2},{4,5},{5,4},{6,7},{7,6},{8,9},{9,8},{10,11... | collective-permute-start | bytes 786440 | tf_op jit(solution)/shard_map/ppermute | solution.py:214
  81.6 7.3 %collective-permute-start.8 = (f32[8,64,128]{2,1,0:T(8,128)S(1)}, f32[8,64,128]{2,1,0:T(8,128)S(1)}, u32[]{:S(2)}, u32[]{:S(2)}) collective-permute-start(f32[8,64,128]{2,1,0:T(8,128)S(1)} %get-tuple-element.65), channel_id=1, source_target_pairs={{0,1},{1,0},{2,3},{3,2},{4,5},{5,4},{6,7},{7,6},{8,9},{9,8},{10,11... | collective-permute-start | bytes 786440 | tf_op jit(solution)/shard_map/ppermute | solution.py:214
  85.0 6.3 %collective-permute-start.3 = (f32[8,64,128]{2,1,0:T(8,128)S(1)}, f32[8,64,128]{2,1,0:T(8,128)S(1)}, u32[]{:S(2)}, u32[]{:S(2)}) collective-permute-start(f32[8,64,128]{2,1,0:T(8,128)S(1)} %get-tuple-element.55), channel_id=1, source_target_pairs={{0,1},{1,0},{2,3},{3,2},{4,5},{5,4},{6,7},{7,6},{8,9},{9,8},{10,11... | collective-permute-start | bytes 786440 | tf_op jit(solution)/shard_map/ppermute | solution.py:214
  85.9 9.2 %collective-permute-start.19 = (f32[8,64,128]{2,1,0:T(8,128)S(1)}, f32[8,64,128]{2,1,0:T(8,128)S(1)}, u32[]{:S(2)}, u32[]{:S(2)}) collective-permute-start(f32[8,64,128]{2,1,0:T(8,128)S(1)} %get-tuple-element.87), channel_id=1, source_target_pairs={{0,2},{1,3},{2,0},{3,1},{4,6},{5,7},{6,4},{7,5},{8,10},{9,11},{10,... | collective-permute-start | bytes 786440 | tf_op jit(solution)/shard_map/ppermute | solution.py:214
  88.3 12.5 %collective-permute-start.14 = (f32[8,64,128]{2,1,0:T(8,128)S(1)}, f32[8,64,128]{2,1,0:T(8,128)S(1)}, u32[]{:S(2)}, u32[]{:S(2)}) collective-permute-start(f32[8,64,128]{2,1,0:T(8,128)S(1)} %get-tuple-element.77), channel_id=1, source_target_pairs={{0,2},{1,3},{2,0},{3,1},{4,6},{5,7},{6,4},{7,5},{8,10},{9,11},{10,... | collective-permute-start | bytes 786440 | tf_op jit(solution)/shard_map/ppermute | solution.py:214
  89.7 16.7 %collective-permute-start.9 = (f32[8,64,128]{2,1,0:T(8,128)S(1)}, f32[8,64,128]{2,1,0:T(8,128)S(1)}, u32[]{:S(2)}, u32[]{:S(2)}) collective-permute-start(f32[8,64,128]{2,1,0:T(8,128)S(1)} %get-tuple-element.67), channel_id=1, source_target_pairs={{0,2},{1,3},{2,0},{3,1},{4,6},{5,7},{6,4},{7,5},{8,10},{9,11},{10,... | collective-permute-start | bytes 786440 | tf_op jit(solution)/shard_map/ppermute | solution.py:214
  92.1 19.4 %collective-permute-start.4 = (f32[8,64,128]{2,1,0:T(8,128)S(1)}, f32[8,64,128]{2,1,0:T(8,128)S(1)}, u32[]{:S(2)}, u32[]{:S(2)}) collective-permute-start(f32[8,64,128]{2,1,0:T(8,128)S(1)} %get-tuple-element.57), channel_id=1, source_target_pairs={{0,2},{1,3},{2,0},{3,1},{4,6},{5,7},{6,4},{7,5},{8,10},{9,11},{10,... | collective-permute-start | bytes 786440 | tf_op jit(solution)/shard_map/ppermute | solution.py:214

commit v2 on v1

v2 whole, which is shorter than its diff:
```python
import functools
import math

import jax
import jax.numpy as jnp
from jax import lax
from jax.experimental import pallas as pl
from jax.experimental.pallas import tpu as pltpu
from jax.sharding import PartitionSpec as P

ROWS_DEV = 16
BOXES = 9
LANES = 128
HALF = ROWS_DEV // 2


LANE_BITS = LANES.bit_length() - 1


def padding(longest_shift):
    return -(-(longest_shift // LANES + 1) // 8) * 8


def bit_of(number, position):
    return lax.shift_right_logical(number, jnp.int32(position)) & 1


class Ratio:
    def __init__(self, low, both, top):
        self.both = both
        self.powers = [(jnp.int32(0), low)]
        for _ in range(top - 1):
            self.powers.append(self.add(self.powers[-1], self.powers[-1]))

    def add(self, one, two):
        rest = one[1] + two[1]
        over = rest >= self.both
        whole = one[0] + two[0]
        return jnp.where(over, whole + 1, whole), jnp.where(over, rest - self.both, rest)

    def scaled(self, power, factor):
        whole, rest = self.powers[power]
        return whole * factor, rest * factor


def delayed(source, row, shift, pad, tiles):
    coarse = lax.shift_right_logical(shift, jnp.int32(LANE_BITS))
    fine = shift & (LANES - 1)
    here = source[row, pl.ds(pad - coarse, tiles), :]
    before = source[row, pl.ds(pad - coarse - 1, tiles), :]
    lane = lax.broadcasted_iota(jnp.int32, (tiles, LANES), 1)
    mixed = jnp.where(lane < LANES - fine, here, before)
    return pltpu.roll(mixed, fine, 1)


class Plan:
    def __init__(self, bits, row_bits, order):
        self.bits, self.row_bits, self.order = bits, row_bits, order

    def free(self, merged, exchanged):
        return [p for p in range(self.row_bits + merged) if p not in exchanged]

    def stage(self, count):
        merged, open_bits = 0, []
        for position in range(count):
            open_bits = [self.order[position]] + open_bits
            if position < count - 1:
                while merged in open_bits:
                    open_bits = [p for p in open_bits if p != merged]
                    merged += 1
        return merged, open_bits


def row_tables(plan, info, merged, sources, exchanged):
    device = info[0]
    base = device
    for position, value in sources.items():
        base = (base & ~(1 << position)) | (value << position)
    size = 2**merged
    first = lax.shift_right_logical(base, jnp.int32(merged + 1)) * (2 * size)
    low = info[1 + first + size] - info[1 + first]
    both = info[1 + first + 2 * size] - info[1 + first]
    total = plan.row_bits + merged + 1
    ratio = Ratio(low, both, total)
    start = (jnp.int32(0), jnp.int32(0))
    for position in range(total):
        if position in exchanged:
            start = ratio.add(start, ratio.scaled(total - 1 - position, bit_of(device, position)))
    table = [start]
    for position in range(total):
        if position not in exchanged:
            power = ratio.powers[total - 1 - position]
            table = [value for old in table for value in (old, ratio.add(old, power))]
    return [value[0] for value in table]


def place(open_bits, sources):
    index = 0
    for position in open_bits:
        index = 2 * index + sources[position]
    return index


def combos(open_bits):
    result = [{}]
    for position in open_bits:
        result = [{**old, position: value} for old in result for value in (0, 1)]
    return result


def merge_all(plan, tiles, pad, info, merged, open_bits, exchanged, held, other):
    source, target = held, other
    while True:
        rows = 2 ** (plan.row_bits - len(open_bits))
        if merged not in open_bits:
            def plain(sources, index, shift=None, source=source, open_bits=open_bits, rows=rows):
                return source[place(open_bits, sources) * rows + index, pad : pad + tiles, :]

            return open_bits, merged, plain, None
        left = [p for p in open_bits if p != merged]
        tables = {}
        for number, sources in enumerate(combos(left)):
            tables[number] = row_tables(plan, info, merged, sources, exchanged)

        def row(sources, index, shift, source=source, open_bits=open_bits, rows=rows, merged=merged):
            low = place(open_bits, {**sources, merged: 0}) * rows
            high = place(open_bits, {**sources, merged: 1}) * rows
            half = lax.shift_right_logical(index, jnp.int32(1)) if hasattr(index, "dtype") else index // 2
            return source[low + half, pad : pad + tiles, :] + delayed(
                source, high + half, shift, pad, tiles
            )

        if merged + 1 not in left:
            return left, merged + 1, row, tables
        for number, sources in enumerate(combos(left)):
            for index in range(2 * rows):
                target[number * 2 * rows + index, pad : pad + tiles, :] = row(
                    sources, index, tables[number][index]
                )
        source, target = target, source
        open_bits, merged = left, merged + 1


def emit_halves(plan, info, merged, open_bits, exchanged, following, row, tables, keep, send):
    mine = bit_of(info[0], following)
    free = plan.free(merged, exchanged)
    weight = 2 ** (len(free) - 1 - free.index(following))
    count = 2 ** len(free)
    for number, sources in enumerate(combos(open_bits)):
        for half, ref in ((1 - mine, send), (mine, keep)):
            slot = 0
            for index in range(count):
                if index & weight:
                    continue
                shift = None
                if tables is not None:
                    shift = jnp.where(half == 1, tables[number][index + weight], tables[number][index])
                ref[number * (count // 2) + slot] = row(sources, index + half * weight, shift)
                slot += 1


def local_kernel(plan, beam, chan_dev, tiles, pad, parts, info, spans, sums, power, keep, send, *scratch):
    stage, wide, level_a, level_b, sems = scratch
    piece = tiles * LANES // parts
    copies = []
    for part in range(parts):
        columns = pl.ds(part * piece, piece)
        copies.append(
            pltpu.make_async_copy(
                power.at[beam, :, columns], stage.at[:, columns], sems.at[part]
            )
        )
        copies[-1].start()
    device = info[0]
    groups = HALF
    span = chan_dev // groups
    zero = jnp.zeros((pad, LANES), jnp.float32)
    for m in range(2 * HALF):
        level_a[m, 0:pad, :] = zero
        level_b[m, 0:pad, :] = zero
    widths = []
    for m in range(groups):
        total = spans[device * chan_dev + m * span]
        for c in range(1, span):
            total = total + spans[device * chan_dev + m * span + c]
        widths.append(total)
    for part in range(parts):
        copies[part].wait()
        value = jnp.dot(
            sums[...],
            stage[:, part * piece : (part + 1) * piece],
            preferred_element_type=jnp.float32,
        )
        for tile in range(piece // LANES):
            wide[part * (piece // LANES) + tile] = value[:, tile * LANES : (tile + 1) * LANES]
    for m in range(1, groups, 2):
        level_a[m, pad : pad + tiles, :] = wide[:, m, :]
    source, target = level_a, level_b
    rows = 4
    bands = groups // 2
    old_rows = 1

    def low_row(m, q):
        if old_rows == 1:
            return wide[:, m, :]
        return source[m * old_rows + q, pad : pad + tiles, :]

    def shifts_of(low, both):
        ratio = Ratio(low, both, max(1, (rows - 1).bit_length()))
        table = [(jnp.int32(0), jnp.int32(0))]
        for power in reversed(ratio.powers):
            table = [value for old in table for value in (old, ratio.add(old, power))]
        return [value[0] for value in table]

    while rows < ROWS_DEV:
        merged = []
        for m in range(bands):
            low, both = widths[2 * m], widths[2 * m] + widths[2 * m + 1]
            merged.append(both)
            shifts = shifts_of(low, both)
            for r in range(rows):
                q = r * old_rows // rows
                high = (2 * m + 1) * old_rows + q
                result = low_row(2 * m, q)
                if r < 2:
                    result = result + source[high, pad : pad + tiles, :]
                else:
                    result = result + delayed(source, high, shifts[r], pad, tiles)
                target[m * rows + r, pad : pad + tiles, :] = result
        widths = merged
        source, target = target, source
        old_rows, rows, bands = rows, rows * 2, bands // 2
    tables = {0: shifts_of(widths[0], widths[0] + widths[1])}

    def row(sources, index, shift):
        half = lax.shift_right_logical(index, jnp.int32(1))
        return source[half, pad : pad + tiles, :] + delayed(source, HALF + half, shift, pad, tiles)

    emit_halves(plan, info, 0, [], [], plan.order[0], row, tables, keep, send)


def fetch(plan, count, tiles, pad, info, kept, came, held, other):
    mine = bit_of(info[0], plan.order[count - 1])
    zero = jnp.zeros((pad, LANES), jnp.float32)
    for q in range(2 * HALF):
        held[q, 0:pad, :] = zero
        if other is not None:
            other[q, 0:pad, :] = zero
    for q in range(HALF):
        held[mine * HALF + q, pad : pad + tiles, :] = kept[q]
        held[(1 - mine) * HALF + q, pad : pad + tiles, :] = came[q]


def merge_kernel(plan, count, tiles, pad, info, kept, came, after, keep, send, held, other):
    del after
    merged, open_bits = plan.stage(count)
    exchanged = plan.order[:count]
    fetch(plan, count, tiles, pad, info, kept, came, held, other)
    open_bits, merged, row, tables = merge_all(
        plan, tiles, pad, info, merged, open_bits, exchanged, held, other
    )
    emit_halves(
        plan, info, merged, open_bits, exchanged, plan.order[count], row, tables, keep, send
    )


def final_kernel(plan, beam, tiles, pad, scale, *refs):
    info, kept, came = refs[:3]
    plane, peak, held, other, run_a, run_b, best, out_plane, out_peak, sems = refs[-10:]
    count = plan.bits
    merged, open_bits = plan.stage(count)
    fetch(plan, count, tiles, pad, info, kept, came, held, other)
    _, _, row, tables = merge_all(
        plan, tiles, pad, info, merged, open_bits, plan.order, held, other
    )
    lane = lax.broadcasted_iota(jnp.int32, (tiles, LANES), 1)
    zero = jnp.zeros((8, LANES), jnp.float32)
    copies = []
    for group in range(0, ROWS_DEV, 8):
        for i in range(8):
            run_a[i, 0:8, :] = zero
            run_b[i, 0:8, :] = zero
            value = row({}, group + i, tables[0][group + i]) * scale
            run_a[i, 8 : 8 + tiles, :] = value
            best[i] = value
        for j in range(tiles):
            out_plane[group : group + 8, j * LANES : (j + 1) * LANES] = run_a[:, 8 + j, :]
        copies.append(
            pltpu.make_async_copy(
                out_plane.at[pl.ds(group, 8)], plane.at[beam, pl.ds(group, 8)], sems.at[0, group // 8]
            )
        )
        copies[-1].start()
        source, target = run_a, run_b
        width = 1
        for level in range(BOXES - 1):
            for i in range(8):
                here = source[i, 8 : 8 + tiles, :]
                before = source[i, 7 : 7 + tiles, :]
                if width < LANES:
                    moved = pltpu.roll(jnp.where(lane < LANES - width, here, before), width, 1)
                else:
                    moved = before
                value = here + moved
                target[i, 8 : 8 + tiles, :] = value
                best[i] = jnp.maximum(best[i], value * (1.0 / math.sqrt(2 * width)))
            source, target = target, source
            width = width * 2
        for j in range(tiles):
            out_peak[group : group + 8, j * LANES : (j + 1) * LANES] = best[:, j, :]
        copies.append(
            pltpu.make_async_copy(
                out_peak.at[pl.ds(group, 8)], peak.at[beam, pl.ds(group, 8)], sems.at[1, group // 8]
            )
        )
        copies[-1].start()
    for copy in copies:
        copy.wait()


SMEM = pl.BlockSpec(memory_space=pltpu.SMEM)
VMEM = pl.BlockSpec(memory_space=pltpu.VMEM)
HBM = pl.BlockSpec(memory_space=pltpu.HBM)
ANY = pl.BlockSpec(memory_space=pl.ANY)


def swapped(value, axis, distance):
    mask = 2**distance
    return lax.ppermute(value, axis, [(s, s ^ mask) for s in range(lax.axis_size(axis))])


def allowed(wanted):
    left, order, merged = list(wanted), [], 0
    while left:
        bit = next(p for p in left if p < ROWS_DEV.bit_length() - 1 + merged)
        left.remove(bit)
        order.append(bit)
        while merged in order:
            merged += 1
    return order


def arrangement(bits, sub_bits, beams):
    far = sub_bits - 1
    near = list(range(far))
    rest = list(range(sub_bits, bits))
    kinds = [
        [far] + near + rest,
        near[:1] + [far] + near[1:] + rest,
        near + [far] + rest,
        near[:1] + rest[-1:] + near[1:] + rest[:-1] + [far],
    ]
    orders = [allowed(kinds[beam % len(kinds)]) for beam in range(beams)]
    schedule = [(beam, count) for count in range(bits + 1) for beam in range(beams)]
    return orders, schedule


def on_device(intensity, channel_spans):
    beams, chan_dev, samples = intensity.shape
    sub_count = lax.axis_size("sub")
    band_size = lax.axis_size("band")
    devices = sub_count * band_size
    tiles = samples // LANES
    sub_bits = sub_count.bit_length() - 1
    bits = devices.bit_length() - 1
    device = lax.axis_index("band") * sub_count + lax.axis_index("sub")
    totals = channel_spans.reshape(devices, chan_dev).sum(axis=1)
    edge = jnp.arange(devices + 1)[:, None] > jnp.arange(devices)[None, :]
    edges = jnp.where(edge, totals[None, :], 0).sum(axis=1)
    info = jnp.concatenate([device.reshape(1), edges]).astype(jnp.int32)
    spot = device.reshape(1).astype(jnp.int32)
    group = jnp.arange(chan_dev) // (chan_dev // HALF)
    sums = (jnp.arange(HALF)[:, None] == group[None, :]).astype(jnp.bfloat16)
    halves = jax.ShapeDtypeStruct((HALF, tiles, LANES), jnp.float32)
    whole = jax.ShapeDtypeStruct((beams, ROWS_DEV, samples), jnp.float32)
    size = HALF * tiles * LANES
    parts = 4

    row_bits = ROWS_DEV.bit_length() - 1
    orders, schedule = arrangement(bits, sub_bits, beams)
    plans = [Plan(bits, row_bits, order) for order in orders]
    pads = padding(ROWS_DEV * 2**bits)

    def local(beam, after):
        del after
        pad = padding(ROWS_DEV)
        padded = pltpu.VMEM((2 * HALF, pad + tiles, LANES), jnp.float32)
        return pl.pallas_call(
            functools.partial(local_kernel, plans[beam], beam, chan_dev, tiles, pad, parts),
            in_specs=[SMEM, SMEM, VMEM, HBM],
            out_specs=[VMEM, VMEM],
            out_shape=[halves, halves],
            scratch_shapes=[
                pltpu.VMEM((chan_dev, samples), jnp.bfloat16),
                pltpu.VMEM((tiles, HALF, LANES), jnp.float32),
                padded,
                padded,
                pltpu.SemaphoreType.DMA((parts,)),
            ],
            compiler_params=pltpu.CompilerParams(vmem_limit_bytes=12 << 20),
            cost_estimate=pl.CostEstimate(
                flops=size * 40, bytes_accessed=chan_dev * samples * 2 + size * 8, transcendentals=0
            ),
            name="local",
        )(spot, channel_spans, sums, intensity)

    def merge(beam, count, kept, came, after):
        padded = pltpu.VMEM((2 * HALF, pads + tiles, LANES), jnp.float32)
        return pl.pallas_call(
            functools.partial(merge_kernel, plans[beam], count, tiles, pads),
            in_specs=[SMEM, VMEM, VMEM, ANY],
            out_specs=[VMEM, VMEM],
            out_shape=[halves, halves],
            scratch_shapes=[padded, padded],
            compiler_params=pltpu.CompilerParams(vmem_limit_bytes=4 << 20),
            cost_estimate=pl.CostEstimate(
                flops=size * 8, bytes_accessed=size * 16, transcendentals=0
            ),
            name=f"merge{count}_{beam}",
        )(info, kept, came, after)

    def final(beam, kept, came, after, done):
        run = pltpu.VMEM((8, 8 + tiles, LANES), jnp.float32)
        rows = pltpu.VMEM((ROWS_DEV, samples), jnp.float32)
        padded = pltpu.VMEM((2 * HALF, pads + tiles, LANES), jnp.float32)
        extra = [after] if not done else []
        return pl.pallas_call(
            functools.partial(
                final_kernel, plans[beam], beam, tiles, pads, 1.0 / math.sqrt(chan_dev * devices)
            ),
            in_specs=[SMEM, VMEM, VMEM] + [ANY] * len(extra) + [HBM] * len(done),
            out_specs=[HBM, HBM],
            out_shape=[whole, whole],
            scratch_shapes=[
                padded,
                padded,
                run,
                run,
                pltpu.VMEM((8, tiles, LANES), jnp.float32),
                rows,
                rows,
                pltpu.SemaphoreType.DMA((2, ROWS_DEV // 8)),
            ],
            input_output_aliases={3 + i: i for i in range(len(done))},
            compiler_params=pltpu.CompilerParams(vmem_limit_bytes=12 << 20),
            cost_estimate=pl.CostEstimate(
                flops=size * 80, bytes_accessed=size * 24, transcendentals=0
            ),
            name=f"final_{beam}",
        )(info, kept, came, *extra, *done)

    done, after = (), None
    state, came = {}, {}
    for beam, count in schedule:
        if count == 0:
            kept, send = local(beam, after)
        elif count < bits:
            kept, send = merge(beam, count, state[beam], came[beam], after)
        else:
            done = final(beam, state[beam], came[beam], after, done)
            continue
        after = kept
        state[beam] = kept
        bit = orders[beam][count]
        axis, distance = ("sub", bit) if bit < sub_bits else ("band", bit - sub_bits)
        came[beam] = swapped(send, axis, distance)
    return tuple(done)


def solution(mesh):
    spec = P(None, ("band", "sub"), None)
    return jax.shard_map(
        on_device, mesh=mesh, in_specs=(spec, P()), out_specs=(spec, spec), check_vma=False
    )
```

time: 116 us -> 93.5 us (0.81)
  waiting for transfers between devices: 49.6 us -> 24.4 us
  starting transfers between devices: 22.8 us -> 25.3 us
    ppermute x20, waiting for transfers between devices: 49.6 us -> 24.4 us  [swapped(): lax.ppermute(value, axis, [(s, s ^ mask) for s in range(lax.axis_size(axi...]
    ppermute x20, starting transfers between devices: 22.8 us -> 25.3 us  [swapped(): lax.ppermute(value, axis, [(s, s ^ mask) for s in range(lax.axis_size(axi...]
  transfers between devices with their start and end apart: 20 -> 20, of which waited for: 11 -> 10; matrix products, arithmetic and copies ran while one was open for 0% -> 0% of each run, Pallas kernels for 27% -> 34%
where the time goes in v2:
time: 93.5 us; the launch traced here: 93.2 us
  Pallas kernels  38 us (41%)
  starting transfers between devices  25.3 us (27%)
  waiting for transfers between devices  24.4 us (26%)
  local copies, waits for them, and re-layouts  4.09 us (4%)
  between operations  1.08 us (1%)
    ppermute x20, starting transfers between devices, swapped(): lax.ppermute(value, axis, [(s, s ^ mask) for s in range(lax.axis_size(axi...  25.3 us
    ppermute x20, waiting for transfers between devices, swapped(): lax.ppermute(value, axis, [(s, s ^ mask) for s in range(lax.axis_size(axi...  24.4 us
    pallas_call x4, Pallas kernels, final(): pl.pallas_call(functools.partial(final_kernel, plans[beam], beam, tiles,...  15.2 us
    pallas_call x16, Pallas kernels, merge(): pl.pallas_call(functools.partial(merge_kernel, plans[beam], count, tiles,...  12.6 us
    pallas_call x4, Pallas kernels, local(): pl.pallas_call(functools.partial(local_kernel, plans[beam], beam, chan_de...  10.2 us
    unnamed x4, local copies, waits for them, and re-layouts  4.09 us
  transfers between devices with their start and end apart: 20, of which 10 were waited for; matrix products, arithmetic and copies ran while one was open for 0% of the time, Pallas kernels for 34%

profile of v2, /device:TPU:0, one launch (start us, length us, event | category | flops | bytes accessed | tf_op | source)
XLA Modules:
  0.0 93.2 jit_solution(14242701211976148416)
XLA Ops:
  0.7 3.4 %copy-done = bf16[4,128,8192]{2,1,0:T(8,128)(2,1)S(1)} copy-done((bf16[4,128,8192]{2,1,0:T(8,128)(2,1)S(1)}, bf16[4,128,8192]{2,1,0:T(8,128)(2,1)}, u32[]{:S(2)}) %copy-start) | copy-done | bytes 8388632
  4.1 0.7 copy-done.1
  4.8 2.5 %local.7 = (f32[8,64,128]{2,1,0:T(8,128)S(1)}, f32[8,64,128]{2,1,0:T(8,128)S(1)}) custom-call(s32[1]{0:T(128)} %bitcast.info, s32[4096]{0:T(1024)S(1)} %copy-done.1, bf16[8,128]{1,0:T(8,128)(2,1)S(1)} %fusion.sums, bf16[4,128,8192]{2,1,0:T(8,128)(2,1)S(1)} %copy-done), custom_call_target="tpu_custom_call" | custom-call | flops 2621440 | bytes 2621440 | tf_op jit(solution)/shard_map/local/pallas_call | solution.py:388
  7.3 4.1 %collective-permute-start.3 = (f32[8,64,128]{2,1,0:T(8,128)S(1)}, f32[8,64,128]{2,1,0:T(8,128)S(1)}, u32[]{:S(2)}, u32[]{:S(2)}) collective-permute-start(f32[8,64,128]{2,1,0:T(8,128)S(1)} %get-tuple-element.55), channel_id=1, source_target_pairs={{0,16},{4,20},{8,24},{12,28},{16,0},{20,4},{24,8},{28,12},{1,17},{... | collective-permute-start | bytes 786440 | tf_op jit(solution)/shard_map/ppermute | solution.py:329
  11.4 2.5 %local.6 = (f32[8,64,128]{2,1,0:T(8,128)S(1)}, f32[8,64,128]{2,1,0:T(8,128)S(1)}) custom-call(s32[1]{0:T(128)} %bitcast.info, s32[4096]{0:T(1024)S(1)} %copy-done.1, bf16[8,128]{1,0:T(8,128)(2,1)S(1)} %fusion.sums, bf16[4,128,8192]{2,1,0:T(8,128)(2,1)S(1)} %copy-done), custom_call_target="tpu_custom_call" | custom-call | flops 2621440 | bytes 2621440 | tf_op jit(solution)/shard_map/local/pallas_call | solution.py:388
  13.9 1.6 %collective-permute-start.2 = (f32[8,64,128]{2,1,0:T(8,128)S(1)}, f32[8,64,128]{2,1,0:T(8,128)S(1)}, u32[]{:S(2)}, u32[]{:S(2)}) collective-permute-start(f32[8,64,128]{2,1,0:T(8,128)S(1)} %get-tuple-element.53), channel_id=1, source_target_pairs={{0,4},{4,0},{8,12},{12,8},{16,20},{20,16},{24,28},{28,24},{1,5},{5... | collective-permute-start | bytes 786440 | tf_op jit(solution)/shard_map/ppermute | solution.py:329
  15.5 2.5 %local.5 = (f32[8,64,128]{2,1,0:T(8,128)S(1)}, f32[8,64,128]{2,1,0:T(8,128)S(1)}) custom-call(s32[1]{0:T(128)} %bitcast.info, s32[4096]{0:T(1024)S(1)} %copy-done.1, bf16[8,128]{1,0:T(8,128)(2,1)S(1)} %fusion.sums, bf16[4,128,8192]{2,1,0:T(8,128)(2,1)S(1)} %copy-done), custom_call_target="tpu_custom_call" | custom-call | flops 2621440 | bytes 2621440 | tf_op jit(solution)/shard_map/local/pallas_call | solution.py:388
  18.6 2.7 %local.4 = (f32[8,64,128]{2,1,0:T(8,128)S(1)}, f32[8,64,128]{2,1,0:T(8,128)S(1)}) custom-call(s32[1]{0:T(128)} %bitcast.info, s32[4096]{0:T(1024)S(1)} %copy-done.1, bf16[8,128]{1,0:T(8,128)(2,1)S(1)} %fusion.sums, bf16[4,128,8192]{2,1,0:T(8,128)(2,1)S(1)} %copy-done), custom_call_target="tpu_custom_call" | custom-call | flops 2621440 | bytes 2621440 | tf_op jit(solution)/shard_map/local/pallas_call | solution.py:388
  21.2 1.6 %collective-permute-start = (f32[8,64,128]{2,1,0:T(8,128)S(1)}, f32[8,64,128]{2,1,0:T(8,128)S(1)}, u32[]{:S(2)}, u32[]{:S(2)}) collective-permute-start(f32[8,64,128]{2,1,0:T(8,128)S(1)} %get-tuple-element.49), channel_id=1, source_target_pairs={{0,4},{4,0},{8,12},{12,8},{16,20},{20,16},{24,28},{28,24},{1,5},{5... | collective-permute-start | bytes 786440 | tf_op jit(solution)/shard_map/ppermute | solution.py:329
  23.3 0.6 merge1_0.1
  23.9 1.6 %collective-permute-start.7 = (f32[8,64,128]{2,1,0:T(8,128)S(1)}, f32[8,64,128]{2,1,0:T(8,128)S(1)}, u32[]{:S(2)}, u32[]{:S(2)}) collective-permute-start(f32[8,64,128]{2,1,0:T(8,128)S(1)} %get-tuple-element.63), channel_id=1, source_target_pairs={{0,4},{4,0},{8,12},{12,8},{16,20},{20,16},{24,28},{28,24},{1,5},{5... | collective-permute-start | bytes 786440 | tf_op jit(solution)/shard_map/ppermute | solution.py:329
  25.6 0.8 merge1_1.1
  26.5 2.3 %collective-permute-done.1.came = f32[8,64,128]{2,1,0:T(8,128)S(1)} collective-permute-done((f32[8,64,128]{2,1,0:T(8,128)S(1)}, f32[8,64,128]{2,1,0:T(8,128)S(1)}, u32[]{:S(2)}, u32[]{:S(2)}) %collective-permute-start.1) | collective-permute-done | bytes 262176 | tf_op jit(solution)/shard_map/ppermute | solution.py:329
  28.8 0.8 merge1_2.1
  29.6 1.8 %collective-permute-start.5 = (f32[8,64,128]{2,1,0:T(8,128)S(1)}, f32[8,64,128]{2,1,0:T(8,128)S(1)}, u32[]{:S(2)}, u32[]{:S(2)}) collective-permute-start(f32[8,64,128]{2,1,0:T(8,128)S(1)} %get-tuple-element.61), channel_id=1, source_target_pairs={{0,8},{4,12},{8,0},{12,4},{16,24},{20,28},{24,16},{28,20},{1,9},{5... | collective-permute-start | bytes 786440 | tf_op jit(solution)/shard_map/ppermute | solution.py:329
  31.4 3.0 %collective-permute-done.came = f32[8,64,128]{2,1,0:T(8,128)S(1)} collective-permute-done((f32[8,64,128]{2,1,0:T(8,128)S(1)}, f32[8,64,128]{2,1,0:T(8,128)S(1)}, u32[]{:S(2)}, u32[]{:S(2)}) %collective-permute-start) | collective-permute-done | bytes 262176 | tf_op jit(solution)/shard_map/ppermute | solution.py:329
  34.4 0.8 merge1_3.1
  35.2 1.6 %collective-permute-start.4 = (f32[8,64,128]{2,1,0:T(8,128)S(1)}, f32[8,64,128]{2,1,0:T(8,128)S(1)}, u32[]{:S(2)}, u32[]{:S(2)}) collective-permute-start(f32[8,64,128]{2,1,0:T(8,128)S(1)} %get-tuple-element.60), channel_id=1, source_target_pairs={{0,2},{1,3},{2,0},{3,1},{4,6},{5,7},{6,4},{7,5},{8,10},{9,11},{10,... | collective-permute-start | bytes 786440 | tf_op jit(solution)/shard_map/ppermute | solution.py:329
  36.7 1.9 %collective-permute-done.7.came = f32[8,64,128]{2,1,0:T(8,128)S(1)} collective-permute-done((f32[8,64,128]{2,1,0:T(8,128)S(1)}, f32[8,64,128]{2,1,0:T(8,128)S(1)}, u32[]{:S(2)}, u32[]{:S(2)}) %collective-permute-start.7) | collective-permute-done | bytes 262176 | tf_op jit(solution)/shard_map/ppermute | solution.py:329
  38.6 0.8 merge2_0.1
  39.4 1.6 %collective-permute-start.11 = (f32[8,64,128]{2,1,0:T(8,128)S(1)}, f32[8,64,128]{2,1,0:T(8,128)S(1)}, u32[]{:S(2)}, u32[]{:S(2)}) collective-permute-start(f32[8,64,128]{2,1,0:T(8,128)S(1)} %get-tuple-element.71), channel_id=1, source_target_pairs={{0,8},{4,12},{8,0},{12,4},{16,24},{20,28},{24,16},{28,20},{1,9},{5... | collective-permute-start | bytes 786440 | tf_op jit(solution)/shard_map/ppermute | solution.py:329
  41.1 0.6 merge2_1.1
  42.2 0.8 merge2_2.1
  43.0 1.6 %collective-permute-start.9 = (f32[8,64,128]{2,1,0:T(8,128)S(1)}, f32[8,64,128]{2,1,0:T(8,128)S(1)}, u32[]{:S(2)}, u32[]{:S(2)}) collective-permute-start(f32[8,64,128]{2,1,0:T(8,128)S(1)} %get-tuple-element.69), channel_id=1, source_target_pairs={{0,16},{4,20},{8,24},{12,28},{16,0},{20,4},{24,8},{28,12},{1,17},{... | collective-permute-start | bytes 786440 | tf_op jit(solution)/shard_map/ppermute | solution.py:329
  44.6 0.6 merge2_3.1
  45.3 2.5 %collective-permute-start.8 = (f32[8,64,128]{2,1,0:T(8,128)S(1)}, f32[8,64,128]{2,1,0:T(8,128)S(1)}, u32[]{:S(2)}, u32[]{:S(2)}) collective-permute-start(f32[8,64,128]{2,1,0:T(8,128)S(1)} %get-tuple-element.68), channel_id=1, source_target_pairs={{0,8},{4,12},{8,0},{12,4},{16,24},{20,28},{24,16},{28,20},{1,9},{5... | collective-permute-start | bytes 786440 | tf_op jit(solution)/shard_map/ppermute | solution.py:329
  47.8 6.5 %collective-permute-done.11.came = f32[8,64,128]{2,1,0:T(8,128)S(1)} collective-permute-done((f32[8,64,128]{2,1,0:T(8,128)S(1)}, f32[8,64,128]{2,1,0:T(8,128)S(1)}, u32[]{:S(2)}, u32[]{:S(2)}) %collective-permute-start.11) | collective-permute-done | bytes 262176 | tf_op jit(solution)/shard_map/ppermute | solution.py:329
  54.3 1.0 %merge3_0.1 = (f32[8,64,128]{2,1,0:T(8,128)S(1)}, f32[8,64,128]{2,1,0:T(8,128)S(1)}) custom-call(s32[34]{0:T(128)S(1)} %pad_add_fusion.info.refs_0_, f32[8,64,128]{2,1,0:T(8,128)S(1)} %get-tuple-element.64.after.kept, f32[8,64,128]{2,1,0:T(8,128)S(1)} %collective-permute-done.11.came, f32[8,64,128]{2,1,0:T(8,128)S(1)} %get-tuple-element.67.after.kept), custom_call_target="tpu_custom_call" | custom-call | flops 524288 | bytes 1048576 | tf_op jit(solution)/shard_map/merge3_0/pallas_call | solution.py:409
  55.4 4.5 %collective-permute-done.10.came = f32[8,64,128]{2,1,0:T(8,128)S(1)} collective-permute-done((f32[8,64,128]{2,1,0:T(8,128)S(1)}, f32[8,64,128]{2,1,0:T(8,128)S(1)}, u32[]{:S(2)}, u32[]{:S(2)}) %collective-permute-start.10) | collective-permute-done | bytes 262176 | tf_op jit(solution)/shard_map/ppermute | solution.py:329
  59.9 1.0 %merge3_1.1 = (f32[8,64,128]{2,1,0:T(8,128)S(1)}, f32[8,64,128]{2,1,0:T(8,128)S(1)}) custom-call(s32[34]{0:T(128)S(1)} %pad_add_fusion.info.refs_0_, f32[8,64,128]{2,1,0:T(8,128)S(1)} %get-tuple-element.65.after.kept, f32[8,64,128]{2,1,0:T(8,128)S(1)} %collective-permute-done.10.came, f32[8,64,128]{2,1,0:T(8,128)S(1)} %get-tuple-element.72.after.kept), custom_call_target="tpu_custom_call" | custom-call | flops 524288 | bytes 1048576 | tf_op jit(solution)/shard_map/merge3_1/pallas_call | solution.py:409
  61.0 0.8 merge3_2.1
  62.4 1.1 %collective-permute-done.8.came = f32[8,64,128]{2,1,0:T(8,128)S(1)} collective-permute-done((f32[8,64,128]{2,1,0:T(8,128)S(1)}, f32[8,64,128]{2,1,0:T(8,128)S(1)}, u32[]{:S(2)}, u32[]{:S(2)}) %collective-permute-start.8) | collective-permute-done | bytes 262176 | tf_op jit(solution)/shard_map/ppermute | solution.py:329
  63.4 0.8 merge3_3.1
  64.4 0.8 merge4_0.1
  65.2 1.6 %collective-permute-start.19 = (f32[8,64,128]{2,1,0:T(8,128)S(1)}, f32[8,64,128]{2,1,0:T(8,128)S(1)}, u32[]{:S(2)}, u32[]{:S(2)}) collective-permute-start(f32[8,64,128]{2,1,0:T(8,128)S(1)} %get-tuple-element.87), channel_id=1, source_target_pairs={{0,2},{1,3},{2,0},{3,1},{4,6},{5,7},{6,4},{7,5},{8,10},{9,11},{10,... | collective-permute-start | bytes 786440 | tf_op jit(solution)/shard_map/ppermute | solution.py:329
  66.7 0.8 merge4_1.1
  67.5 0.6 collective-permute-start.18
  68.2 0.8 merge4_2.1
  69.0 1.6 %collective-permute-start.17 = (f32[8,64,128]{2,1,0:T(8,128)S(1)}, f32[8,64,128]{2,1,0:T(8,128)S(1)}, u32[]{:S(2)}, u32[]{:S(2)}) collective-permute-start(f32[8,64,128]{2,1,0:T(8,128)S(1)} %get-tuple-element.85), channel_id=1, source_target_pairs={{0,2},{1,3},{2,0},{3,1},{4,6},{5,7},{6,4},{7,5},{8,10},{9,11},{10,... | collective-permute-start | bytes 786440 | tf_op jit(solution)/shard_map/ppermute | solution.py:329
  70.5 0.6 merge4_3.1
  71.2 1.6 %collective-permute-start.16 = (f32[8,64,128]{2,1,0:T(8,128)S(1)}, f32[8,64,128]{2,1,0:T(8,128)S(1)}, u32[]{:S(2)}, u32[]{:S(2)}) collective-permute-start(f32[8,64,128]{2,1,0:T(8,128)S(1)} %get-tuple-element.84), channel_id=1, source_target_pairs={{0,16},{4,20},{8,24},{12,28},{16,0},{20,4},{24,8},{28,12},{1,17},{... | collective-permute-start | bytes 786440 | tf_op jit(solution)/shard_map/ppermute | solution.py:329
  72.7 1.7 %collective-permute-done.19.refs_2_ = f32[8,64,128]{2,1,0:T(8,128)S(1)} collective-permute-done((f32[8,64,128]{2,1,0:T(8,128)S(1)}, f32[8,64,128]{2,1,0:T(8,128)S(1)}, u32[]{:S(2)}, u32[]{:S(2)}) %collective-permute-start.19) | collective-permute-done | bytes 262176 | tf_op jit(solution)/shard_map/ppermute | solution.py:329
  74.4 3.7 %final_0.1 = (f32[4,16,8192]{2,1,0:T(8,128)}, f32[4,16,8192]{2,1,0:T(8,128)}) custom-call(s32[34]{0:T(128)S(1)} %pad_add_fusion.info.refs_0_, f32[8,64,128]{2,1,0:T(8,128)S(1)} %get-tuple-element.80.after.refs_1_, f32[8,64,128]{2,1,0:T(8,128)S(1)} %collective-permute-done.19.refs_2_, f32[8,64,128]{2,1,0:T(8,128)S(1)} %get-tuple-element.83.refs_3_.refs_1_), custom_call_target="tpu_custom_call" | custom-call | flops 5242880 | bytes 1572864 | tf_op jit(solution)/shard_map/final_0/pallas_call | solution.py:427
  78.1 1.9 %collective-permute-done.18.refs_2_ = f32[8,64,128]{2,1,0:T(8,128)S(1)} collective-permute-done((f32[8,64,128]{2,1,0:T(8,128)S(1)}, f32[8,64,128]{2,1,0:T(8,128)S(1)}, u32[]{:S(2)}, u32[]{:S(2)}) %collective-permute-start.18) | collective-permute-done | bytes 262176 | tf_op jit(solution)/shard_map/ppermute | solution.py:329
  80.0 3.7 %final_1.1 = (f32[4,16,8192]{2,1,0:T(8,128)}, f32[4,16,8192]{2,1,0:T(8,128)}) custom-call(s32[34]{0:T(128)S(1)} %pad_add_fusion.info.refs_0_, f32[8,64,128]{2,1,0:T(8,128)S(1)} %get-tuple-element.81.after.refs_1_, f32[8,64,128]{2,1,0:T(8,128)S(1)} %collective-permute-done.18.refs_2_, ...), custom_call_target="tpu_custom_call", output_to_operand_aliasing={{0}: (3, {}), {1}: (4, {})} | custom-call | flops 5242880 | bytes 1572864 | tf_op jit(solution)/shard_map/final_1/pallas_call | solution.py:427
  83.7 1.5 %collective-permute-done.17.refs_2_ = f32[8,64,128]{2,1,0:T(8,128)S(1)} collective-permute-done((f32[8,64,128]{2,1,0:T(8,128)S(1)}, f32[8,64,128]{2,1,0:T(8,128)S(1)}, u32[]{:S(2)}, u32[]{:S(2)}) %collective-permute-start.17) | collective-permute-done | bytes 262176 | tf_op jit(solution)/shard_map/ppermute | solution.py:329
  85.2 3.9 %final_2.1 = (f32[4,16,8192]{2,1,0:T(8,128)}, f32[4,16,8192]{2,1,0:T(8,128)}) custom-call(s32[34]{0:T(128)S(1)} %pad_add_fusion.info.refs_0_, f32[8,64,128]{2,1,0:T(8,128)S(1)} %get-tuple-element.82.after.refs_1_, f32[8,64,128]{2,1,0:T(8,128)S(1)} %collective-permute-done.17.refs_2_, ...), custom_call_target="tpu_custom_call", output_to_operand_aliasing={{0}: (3, {}), {1}: (4, {})} | custom-call | flops 5242880 | bytes 1572864 | tf_op jit(solution)/shard_map/final_2/pallas_call | solution.py:427
  89.1 4.0 %final_3.1 = (f32[4,16,8192]{2,1,0:T(8,128)}, f32[4,16,8192]{2,1,0:T(8,128)}) custom-call(s32[34]{0:T(128)S(1)} %pad_add_fusion.info.refs_0_, f32[8,64,128]{2,1,0:T(8,128)S(1)} %get-tuple-element.83.refs_3_.refs_1_, f32[8,64,128]{2,1,0:T(8,128)S(1)} %collective-permute-done.16.refs_2_, ...), custom_call_target="tpu_custom_call", output_to_operand_aliasing={{0}: (3, {}), {1}: (4, {})} | custom-call | flops 5242880 | bytes 1572864 | tf_op jit(solution)/shard_map/final_3/pallas_call | solution.py:427
  (25 shorter events, 2.5 us)
Async XLA Ops:
  0.7 3.4 %copy-start = (bf16[4,128,8192]{2,1,0:T(8,128)(2,1)S(1)}, bf16[4,128,8192]{2,1,0:T(8,128)(2,1)}, u32[]{:S(2)}) copy-start(bf16[4,128,8192]{2,1,0:T(8,128)(2,1)} %power.7) | copy-start | bytes 25165828
  4.1 0.7 copy-start.1
  7.3 16.0 %collective-permute-start.3 = (f32[8,64,128]{2,1,0:T(8,128)S(1)}, f32[8,64,128]{2,1,0:T(8,128)S(1)}, u32[]{:S(2)}, u32[]{:S(2)}) collective-permute-start(f32[8,64,128]{2,1,0:T(8,128)S(1)} %get-tuple-element.55), channel_id=1, source_target_pairs={{0,16},{4,20},{8,24},{12,28},{16,0},{20,4},{24,8},{28,12},{1,17},{... | collective-permute-start | bytes 786440 | tf_op jit(solution)/shard_map/ppermute | solution.py:329
  13.9 11.7 %collective-permute-start.2 = (f32[8,64,128]{2,1,0:T(8,128)S(1)}, f32[8,64,128]{2,1,0:T(8,128)S(1)}, u32[]{:S(2)}, u32[]{:S(2)}) collective-permute-start(f32[8,64,128]{2,1,0:T(8,128)S(1)} %get-tuple-element.53), channel_id=1, source_target_pairs={{0,4},{4,0},{8,12},{12,8},{16,20},{20,16},{24,28},{28,24},{1,5},{5... | collective-permute-start | bytes 786440 | tf_op jit(solution)/shard_map/ppermute | solution.py:329
  18.0 10.8 %collective-permute-start.1 = (f32[8,64,128]{2,1,0:T(8,128)S(1)}, f32[8,64,128]{2,1,0:T(8,128)S(1)}, u32[]{:S(2)}, u32[]{:S(2)}) collective-permute-start(f32[8,64,128]{2,1,0:T(8,128)S(1)} %get-tuple-element.51), channel_id=1, source_target_pairs={{0,4},{4,0},{8,12},{12,8},{16,20},{20,16},{24,28},{28,24},{1,5},{5... | collective-permute-start | bytes 786440 | tf_op jit(solution)/shard_map/ppermute | solution.py:329
  21.2 13.1 %collective-permute-start = (f32[8,64,128]{2,1,0:T(8,128)S(1)}, f32[8,64,128]{2,1,0:T(8,128)S(1)}, u32[]{:S(2)}, u32[]{:S(2)}) collective-permute-start(f32[8,64,128]{2,1,0:T(8,128)S(1)} %get-tuple-element.49), channel_id=1, source_target_pairs={{0,4},{4,0},{8,12},{12,8},{16,20},{20,16},{24,28},{28,24},{1,5},{5... | collective-permute-start | bytes 786440 | tf_op jit(solution)/shard_map/ppermute | solution.py:329
  23.9 14.6 %collective-permute-start.7 = (f32[8,64,128]{2,1,0:T(8,128)S(1)}, f32[8,64,128]{2,1,0:T(8,128)S(1)}, u32[]{:S(2)}, u32[]{:S(2)}) collective-permute-start(f32[8,64,128]{2,1,0:T(8,128)S(1)} %get-tuple-element.63), channel_id=1, source_target_pairs={{0,4},{4,0},{8,12},{12,8},{16,20},{20,16},{24,28},{28,24},{1,5},{5... | collective-permute-start | bytes 786440 | tf_op jit(solution)/shard_map/ppermute | solution.py:329
  26.4 14.7 %collective-permute-start.6 = (f32[8,64,128]{2,1,0:T(8,128)S(1)}, f32[8,64,128]{2,1,0:T(8,128)S(1)}, u32[]{:S(2)}, u32[]{:S(2)}) collective-permute-start(f32[8,64,128]{2,1,0:T(8,128)S(1)} %get-tuple-element.62), channel_id=1, source_target_pairs={{0,16},{4,20},{8,24},{12,28},{16,0},{20,4},{24,8},{28,12},{1,17},{... | collective-permute-start | bytes 786440 | tf_op jit(solution)/shard_map/ppermute | solution.py:329
  29.6 12.6 %collective-permute-start.5 = (f32[8,64,128]{2,1,0:T(8,128)S(1)}, f32[8,64,128]{2,1,0:T(8,128)S(1)}, u32[]{:S(2)}, u32[]{:S(2)}) collective-permute-start(f32[8,64,128]{2,1,0:T(8,128)S(1)} %get-tuple-element.61), channel_id=1, source_target_pairs={{0,8},{4,12},{8,0},{12,4},{16,24},{20,28},{24,16},{28,20},{1,9},{5... | collective-permute-start | bytes 786440 | tf_op jit(solution)/shard_map/ppermute | solution.py:329
  35.2 9.5 %collective-permute-start.4 = (f32[8,64,128]{2,1,0:T(8,128)S(1)}, f32[8,64,128]{2,1,0:T(8,128)S(1)}, u32[]{:S(2)}, u32[]{:S(2)}) collective-permute-start(f32[8,64,128]{2,1,0:T(8,128)S(1)} %get-tuple-element.60), channel_id=1, source_target_pairs={{0,2},{1,3},{2,0},{3,1},{4,6},{5,7},{6,4},{7,5},{8,10},{9,11},{10,... | collective-permute-start | bytes 786440 | tf_op jit(solution)/shard_map/ppermute | solution.py:329
  39.4 14.9 %collective-permute-start.11 = (f32[8,64,128]{2,1,0:T(8,128)S(1)}, f32[8,64,128]{2,1,0:T(8,128)S(1)}, u32[]{:S(2)}, u32[]{:S(2)}) collective-permute-start(f32[8,64,128]{2,1,0:T(8,128)S(1)} %get-tuple-element.71), channel_id=1, source_target_pairs={{0,8},{4,12},{8,0},{12,4},{16,24},{20,28},{24,16},{28,20},{1,9},{5... | collective-permute-start | bytes 786440 | tf_op jit(solution)/shard_map/ppermute | solution.py:329
  41.7 18.2 %collective-permute-start.10 = (f32[8,64,128]{2,1,0:T(8,128)S(1)}, f32[8,64,128]{2,1,0:T(8,128)S(1)}, u32[]{:S(2)}, u32[]{:S(2)}) collective-permute-start(f32[8,64,128]{2,1,0:T(8,128)S(1)} %get-tuple-element.70), channel_id=1, source_target_pairs={{0,8},{4,12},{8,0},{12,4},{16,24},{20,28},{24,16},{28,20},{1,9},{5... | collective-permute-start | bytes 786440 | tf_op jit(solution)/shard_map/ppermute | solution.py:329
  43.0 18.0 %collective-permute-start.9 = (f32[8,64,128]{2,1,0:T(8,128)S(1)}, f32[8,64,128]{2,1,0:T(8,128)S(1)}, u32[]{:S(2)}, u32[]{:S(2)}) collective-permute-start(f32[8,64,128]{2,1,0:T(8,128)S(1)} %get-tuple-element.69), channel_id=1, source_target_pairs={{0,16},{4,20},{8,24},{12,28},{16,0},{20,4},{24,8},{28,12},{1,17},{... | collective-permute-start | bytes 786440 | tf_op jit(solution)/shard_map/ppermute | solution.py:329
  45.3 18.2 %collective-permute-start.8 = (f32[8,64,128]{2,1,0:T(8,128)S(1)}, f32[8,64,128]{2,1,0:T(8,128)S(1)}, u32[]{:S(2)}, u32[]{:S(2)}) collective-permute-start(f32[8,64,128]{2,1,0:T(8,128)S(1)} %get-tuple-element.68), channel_id=1, source_target_pairs={{0,8},{4,12},{8,0},{12,4},{16,24},{20,28},{24,16},{28,20},{1,9},{5... | collective-permute-start | bytes 786440 | tf_op jit(solution)/shard_map/ppermute | solution.py:329
  55.3 9.0 %collective-permute-start.15 = (f32[8,64,128]{2,1,0:T(8,128)S(1)}, f32[8,64,128]{2,1,0:T(8,128)S(1)}, u32[]{:S(2)}, u32[]{:S(2)}) collective-permute-start(f32[8,64,128]{2,1,0:T(8,128)S(1)} %get-tuple-element.79), channel_id=1, source_target_pairs={{0,1},{1,0},{2,3},{3,2},{4,5},{5,4},{6,7},{7,6},{8,9},{9,8},{10,11... | collective-permute-start | bytes 786440 | tf_op jit(solution)/shard_map/ppermute | solution.py:329
  60.9 5.8 %collective-permute-start.14 = (f32[8,64,128]{2,1,0:T(8,128)S(1)}, f32[8,64,128]{2,1,0:T(8,128)S(1)}, u32[]{:S(2)}, u32[]{:S(2)}) collective-permute-start(f32[8,64,128]{2,1,0:T(8,128)S(1)} %get-tuple-element.78), channel_id=1, source_target_pairs={{0,1},{1,0},{2,3},{3,2},{4,5},{5,4},{6,7},{7,6},{8,9},{9,8},{10,11... | collective-permute-start | bytes 786440 | tf_op jit(solution)/shard_map/ppermute | solution.py:329
  61.8 6.3 %collective-permute-start.13 = (f32[8,64,128]{2,1,0:T(8,128)S(1)}, f32[8,64,128]{2,1,0:T(8,128)S(1)}, u32[]{:S(2)}, u32[]{:S(2)}) collective-permute-start(f32[8,64,128]{2,1,0:T(8,128)S(1)} %get-tuple-element.77), channel_id=1, source_target_pairs={{0,1},{1,0},{2,3},{3,2},{4,5},{5,4},{6,7},{7,6},{8,9},{9,8},{10,11... | collective-permute-start | bytes 786440 | tf_op jit(solution)/shard_map/ppermute | solution.py:329
  64.3 6.3 %collective-permute-start.12 = (f32[8,64,128]{2,1,0:T(8,128)S(1)}, f32[8,64,128]{2,1,0:T(8,128)S(1)}, u32[]{:S(2)}, u32[]{:S(2)}) collective-permute-start(f32[8,64,128]{2,1,0:T(8,128)S(1)} %get-tuple-element.76), channel_id=1, source_target_pairs={{0,1},{1,0},{2,3},{3,2},{4,5},{5,4},{6,7},{7,6},{8,9},{9,8},{10,11... | collective-permute-start | bytes 786440 | tf_op jit(solution)/shard_map/ppermute | solution.py:329
  65.2 9.2 %collective-permute-start.19 = (f32[8,64,128]{2,1,0:T(8,128)S(1)}, f32[8,64,128]{2,1,0:T(8,128)S(1)}, u32[]{:S(2)}, u32[]{:S(2)}) collective-permute-start(f32[8,64,128]{2,1,0:T(8,128)S(1)} %get-tuple-element.87), channel_id=1, source_target_pairs={{0,2},{1,3},{2,0},{3,1},{4,6},{5,7},{6,4},{7,5},{8,10},{9,11},{10,... | collective-permute-start | bytes 786440 | tf_op jit(solution)/shard_map/ppermute | solution.py:329
  67.5 12.5 %collective-permute-start.18 = (f32[8,64,128]{2,1,0:T(8,128)S(1)}, f32[8,64,128]{2,1,0:T(8,128)S(1)}, u32[]{:S(2)}, u32[]{:S(2)}) collective-permute-start(f32[8,64,128]{2,1,0:T(8,128)S(1)} %get-tuple-element.86), channel_id=1, source_target_pairs={{0,2},{1,3},{2,0},{3,1},{4,6},{5,7},{6,4},{7,5},{8,10},{9,11},{10,... | collective-permute-start | bytes 786440 | tf_op jit(solution)/shard_map/ppermute | solution.py:329
  69.0 16.2 %collective-permute-start.17 = (f32[8,64,128]{2,1,0:T(8,128)S(1)}, f32[8,64,128]{2,1,0:T(8,128)S(1)}, u32[]{:S(2)}, u32[]{:S(2)}) collective-permute-start(f32[8,64,128]{2,1,0:T(8,128)S(1)} %get-tuple-element.85), channel_id=1, source_target_pairs={{0,2},{1,3},{2,0},{3,1},{4,6},{5,7},{6,4},{7,5},{8,10},{9,11},{10,... | collective-permute-start | bytes 786440 | tf_op jit(solution)/shard_map/ppermute | solution.py:329
  71.2 17.9 %collective-permute-start.16 = (f32[8,64,128]{2,1,0:T(8,128)S(1)}, f32[8,64,128]{2,1,0:T(8,128)S(1)}, u32[]{:S(2)}, u32[]{:S(2)}) collective-permute-start(f32[8,64,128]{2,1,0:T(8,128)S(1)} %get-tuple-element.84), channel_id=1, source_target_pairs={{0,16},{4,20},{8,24},{12,28},{16,0},{20,4},{24,8},{28,12},{1,17},{... | collective-permute-start | bytes 786440 | tf_op jit(solution)/shard_map/ppermute | solution.py:329
